TPU v7x, 32 devices: a whole 2x2x4 slice. The times are simulated.
32 devices in a mesh: dp: 16 (over z, y, x), fsdp: 2 (over core).
Axes of the slice: x: 2, y: 2, z: 4, core: 2. Of those that a mesh axis runs over, the one named last changes fastest.
Arguments:
- tokens: bfloat16 [4096, 1024], P(('dp', 'fsdp')), may hold values from -6 to 6
- dealing: int32 [4096], P(('dp', 'fsdp')), may hold values from 0 to 4095, as said below
- lengths: int32 [32, 1], P(('dp', 'fsdp')), may hold values from 0 to 128, as said below
- norm1_gain: bfloat16 [1024], P(('dp', 'fsdp')), may hold values from 0.099609375 to 1.8984375
- w_query: bfloat16 [1048576], P(('dp', 'fsdp')), may hold values from -0.1875 to 0.1875
- w_key: bfloat16 [1048576], P(('dp', 'fsdp')), may hold values from -0.1875 to 0.1875
- w_value: bfloat16 [1048576], P(('dp', 'fsdp')), may hold values from -0.1875 to 0.1875
- w_out: bfloat16 [1048576], P(('dp', 'fsdp')), may hold values from -1 to 1
- norm2_gain: bfloat16 [1024], P(('dp', 'fsdp')), may hold values from 0.099609375 to 1.8984375
- w_gate: bfloat16 [2818048], P(('dp', 'fsdp')), may hold values from -0.1875 to 0.1875
- w_up: bfloat16 [2818048], P(('dp', 'fsdp')), may hold values from -0.1875 to 0.1875
- w_down: bfloat16 [2818048], P(('dp', 'fsdp')), may hold values from -0.109375 to 0.109375
- cotangent: bfloat16 [4096, 1024], P(('dp', 'fsdp')), may hold values from -6 to 6
Outputs:
- layer_out: bfloat16 [4096, 1024], P(('dp', 'fsdp'))
- input_grad: bfloat16 [4096, 1024], P(('dp', 'fsdp'))
- grad_norm1_gain: float32 [1024], P(('dp', 'fsdp'))
- grad_w_query: float32 [1048576], P(('dp', 'fsdp'))
- grad_w_key: float32 [1048576], P(('dp', 'fsdp'))
- grad_w_value: float32 [1048576], P(('dp', 'fsdp'))
- grad_w_out: float32 [1048576], P(('dp', 'fsdp'))
- grad_norm2_gain: float32 [1024], P(('dp', 'fsdp'))
- grad_w_gate: float32 [2818048], P(('dp', 'fsdp'))
- grad_w_up: float32 [2818048], P(('dp', 'fsdp'))
- grad_w_down: float32 [2818048], P(('dp', 'fsdp'))
Inputs may be any that keep to these rules, and one draw needn't show every extreme that they name: dealing is a permutation of the dealt indices. The home device with dp index h and fsdp index f holds exactly the dealt indices of the devices with fsdp index f at local positions h * 8 to (h + 1) * 8 - 1, 8 from each such device, in drawn order. `lengths`: each row lists whole sequences that fill its device: entries are multiples of 128, nonzero ones come first and sum to 128; some device holds one sequence of 128 tokens.
All inputs are finite; a program needn't handle non-finite values.
Results may differ from a plain program's by a relative error of at most 0.012.
The roundings to bfloat16 on the way count: a program that leaves them out, or rounds other values in their place, can miss the bound.
Values may be sent and summed in bfloat16 or wider, within the bound.
A program may use at most 256 MiB of HBM per device.

v0:
```python
import jax
import jax.numpy as jnp
from jax import lax
from jax.sharding import PartitionSpec as P

HEAD = 64
WINDOW = 64


EPSILON = 1e-06


def unpack(flat_list, model_width):
    gain_one, query_w, key_w, value_w, out_w, gain_two, gate_w, up_w, down_w = flat_list
    hidden_units = gate_w.shape[0] // model_width
    return (
        gain_one.astype(jnp.float32),
        query_w.reshape(model_width, model_width),
        key_w.reshape(model_width, model_width),
        value_w.reshape(model_width, model_width),
        out_w.reshape(model_width, model_width),
        gain_two.astype(jnp.float32),
        gate_w.reshape(model_width, hidden_units),
        up_w.reshape(model_width, hidden_units),
        down_w.reshape(hidden_units, model_width),
    )


def normalize(values, gain_vec):
    inverse = lax.rsqrt(jnp.mean(values * values, axis=-1, keepdims=True) + EPSILON)
    unit_rows = values * inverse
    return (unit_rows * gain_vec, unit_rows, inverse)


def norm_back(upstream, gain_vec, unit_rows, inverse):
    scaled = upstream * gain_vec
    return inverse * (scaled - unit_rows * jnp.mean(scaled * unit_rows, axis=-1, keepdims=True))


def dot_rows(first_op, second_op):
    return lax.dot_general(
        first_op, second_op, (((0,), (0,)), ((), ())), preferred_element_type=jnp.float32
    )


def dot_back(first_op, second_op):
    return lax.dot_general(
        first_op, second_op, (((1,), (1,)), ((), ())), preferred_element_type=jnp.float32
    )


def flat_piece(entry, count, pieces):
    if entry[0] == "gain":
        vector = entry[1]
        share = vector.shape[0] // pieces
        return vector.reshape(count, share)
    left_op, right_op = (entry[1], entry[2])
    row_total = left_op.shape[1]
    col_total = right_op.shape[1]
    share = row_total * col_total // pieces
    block = dot_rows(left_op, right_op)
    flat = block.reshape(-1)
    return flat.reshape(count, share)


def term_maker(entries, pieces, count):
    return jnp.concatenate([flat_piece(entry, count, pieces) for entry in entries], axis=1)


def split_spans(summed, entries, pieces):
    flat = summed.reshape(-1)
    results = []
    offset = 0
    for entry in entries:
        if entry[0] == "gain":
            share = entry[1].shape[0] // pieces
        else:
            share = entry[1].shape[1] * entry[2].shape[1] // pieces
        results.append(flat[offset : offset + share])
        offset = offset + share
    return results


def block_mask(segment, tok_rows):
    block_count = tok_rows // WINDOW
    padded = jnp.concatenate([jnp.full((WINDOW,), -1, jnp.int32), segment])
    seg_query = segment.reshape(block_count, WINDOW)
    seg_keys = jnp.concatenate([padded[:-WINDOW].reshape(block_count, WINDOW), seg_query], axis=1)
    offset = jnp.arange(WINDOW)[:, None] - jnp.arange(2 * WINDOW)[None, :] + WINDOW
    inside = (offset >= 0) & (offset < WINDOW)
    return inside[None] & (seg_query[:, :, None] == seg_keys[:, None, :])


def key_blocks(values, block_count):
    padded = jnp.concatenate([jnp.zeros((WINDOW,) + values.shape[1:], values.dtype), values])
    previous = padded[:-WINDOW].reshape((block_count, WINDOW) + values.shape[1:])
    current = values.reshape((block_count, WINDOW) + values.shape[1:])
    return jnp.concatenate([previous, current], axis=1)


def fold_keys(key_parts, tok_rows, model_width):
    previous = key_parts[:, :WINDOW]
    current = key_parts[:, WINDOW:]
    shifted = jnp.concatenate([previous[1:], jnp.zeros_like(previous[:1])], axis=0)
    return (current + shifted).reshape(tok_rows, model_width)


def masked_scores(query_blk, key_blk, key_mask):
    scores = jnp.einsum(
        "bahd,bchd->bhac", query_blk, key_blk, preferred_element_type=jnp.float32
    ) * HEAD ** (-0.5)
    return jnp.where(key_mask, scores, -1e30)


def body(
    tokens,
    dealing,
    lengths,
    norm1_gain,
    w_query,
    w_key,
    w_value,
    w_out,
    norm2_gain,
    w_gate,
    w_up,
    w_down,
    cotangent,
):
    tok_rows, model_width = tokens.shape
    dp_count = lax.axis_size("dp")
    fsdp_count = lax.axis_size("fsdp")
    pieces = lax.axis_size(("dp", "fsdp"))
    per_peer = tok_rows // dp_count
    local_pos = dealing % tok_rows
    target_dp = dealing // tok_rows // fsdp_count
    send_slot = target_dp * per_peer + local_pos % per_peer
    sent_tokens = jnp.zeros_like(tokens).at[send_slot].set(tokens)
    sent_cot = jnp.zeros_like(cotangent).at[send_slot].set(cotangent)
    inputs, incoming = (
        lax.all_to_all(sent_tokens, "dp", split_axis=0, concat_axis=0, tiled=True),
        lax.all_to_all(sent_cot, "dp", split_axis=0, concat_axis=0, tiled=True),
    )
    bounds = jnp.cumsum(lengths[0])
    positions = jnp.arange(tok_rows, dtype=jnp.int32)
    segment = jnp.sum((positions[:, None] >= bounds[None, :]).astype(jnp.int32), axis=1)
    block_count = tok_rows // WINDOW
    head_count = model_width // HEAD
    key_mask = block_mask(segment, tok_rows)[:, None]
    flat_weights = (norm1_gain, w_query, w_key, w_value, w_out, norm2_gain, w_gate, w_up, w_down)
    gathered = (
        lax.all_gather(flat_weights[0], ("dp", "fsdp"), axis=0, tiled=True),
        lax.all_gather(flat_weights[1], ("dp", "fsdp"), axis=0, tiled=True),
        lax.all_gather(flat_weights[2], ("dp", "fsdp"), axis=0, tiled=True),
        lax.all_gather(flat_weights[3], ("dp", "fsdp"), axis=0, tiled=True),
        lax.all_gather(flat_weights[4], ("dp", "fsdp"), axis=0, tiled=True),
        lax.all_gather(flat_weights[5], ("dp", "fsdp"), axis=0, tiled=True),
        lax.all_gather(flat_weights[6], ("dp", "fsdp"), axis=0, tiled=True),
        lax.all_gather(flat_weights[7], ("dp", "fsdp"), axis=0, tiled=True),
        lax.all_gather(flat_weights[8], ("dp", "fsdp"), axis=0, tiled=True),
    )
    gain_one, query_w, key_w, value_w, out_w, gain_two, gate_w, up_w, down_w = unpack(
        gathered, model_width
    )
    input_f = inputs.astype(jnp.float32)
    scaled_one, unit_one, inverse_one = normalize(input_f, gain_one)
    normed_one = scaled_one.astype(jnp.bfloat16)
    query_act = jnp.dot(normed_one, query_w, preferred_element_type=jnp.float32).astype(
        jnp.bfloat16
    )
    key_act = jnp.dot(normed_one, key_w, preferred_element_type=jnp.float32).astype(jnp.bfloat16)
    value_act = jnp.dot(normed_one, value_w, preferred_element_type=jnp.float32).astype(
        jnp.bfloat16
    )
    query_blk = query_act.reshape(block_count, WINDOW, head_count, HEAD)
    key_blk = key_blocks(key_act.reshape(tok_rows, head_count, HEAD), block_count)
    value_blk = key_blocks(value_act.reshape(tok_rows, head_count, HEAD), block_count)
    scores = masked_scores(query_blk, key_blk, key_mask)
    row_peak = jnp.max(scores, axis=-1, keepdims=True)
    exp_scores = jnp.exp(scores - row_peak)
    row_total = jnp.sum(exp_scores, axis=-1, keepdims=True)
    log_total = row_peak + jnp.log(row_total)
    probs_low = (exp_scores / row_total).astype(jnp.bfloat16)
    attended = jnp.einsum(
        "bhac,bchd->bahd", probs_low, value_blk, preferred_element_type=jnp.float32
    )
    attended = attended.reshape(tok_rows, model_width).astype(jnp.bfloat16)
    middle = input_f + jnp.dot(attended, out_w, preferred_element_type=jnp.float32)
    scaled_two, unit_two, inverse_two = normalize(middle, gain_two)
    normed_two = scaled_two.astype(jnp.bfloat16)
    gate_pre = jnp.dot(normed_two, gate_w, preferred_element_type=jnp.float32)
    up_pre = jnp.dot(normed_two, up_w, preferred_element_type=jnp.float32)
    sigmoid_gate = jax.nn.sigmoid(gate_pre)
    gate_act = gate_pre * sigmoid_gate
    hidden = (gate_act * up_pre).astype(jnp.bfloat16)
    result = (middle + jnp.dot(hidden, down_w, preferred_element_type=jnp.float32)).astype(
        jnp.bfloat16
    )
    regathered = (
        lax.all_gather(flat_weights[0], ("dp", "fsdp"), axis=0, tiled=True),
        lax.all_gather(flat_weights[1], ("dp", "fsdp"), axis=0, tiled=True),
        lax.all_gather(flat_weights[2], ("dp", "fsdp"), axis=0, tiled=True),
        lax.all_gather(flat_weights[3], ("dp", "fsdp"), axis=0, tiled=True),
        lax.all_gather(flat_weights[4], ("dp", "fsdp"), axis=0, tiled=True),
        lax.all_gather(flat_weights[5], ("dp", "fsdp"), axis=0, tiled=True),
        lax.all_gather(flat_weights[6], ("dp", "fsdp"), axis=0, tiled=True),
        lax.all_gather(flat_weights[7], ("dp", "fsdp"), axis=0, tiled=True),
        lax.all_gather(flat_weights[8], ("dp", "fsdp"), axis=0, tiled=True),
    )
    gain_one, query_w, key_w, value_w, out_w, gain_two, gate_w, up_w, down_w = unpack(
        regathered, model_width
    )
    grad_hidden = dot_back(incoming, down_w)
    grad_gate = (
        grad_hidden * up_pre * sigmoid_gate * (1.0 + gate_pre * (1.0 - sigmoid_gate))
    ).astype(jnp.bfloat16)
    grad_up = (grad_hidden * gate_act).astype(jnp.bfloat16)
    grad_normed_two = dot_back(grad_gate, gate_w) + dot_back(grad_up, up_w)
    grad_gain_two = jnp.sum(grad_normed_two * unit_two, axis=0)
    grad_middle = incoming.astype(jnp.float32) + norm_back(
        grad_normed_two, gain_two, unit_two, inverse_two
    )
    ff_entries = [
        ("gain", grad_gain_two),
        ("mat", normed_two, grad_gate),
        ("mat", normed_two, grad_up),
        ("mat", hidden, incoming),
    ]
    grad_branch = grad_middle.astype(jnp.bfloat16)
    grad_attended = dot_back(grad_branch, out_w).astype(jnp.bfloat16)
    grad_att_blk = grad_attended.reshape(block_count, WINDOW, head_count, HEAD)
    probs = jnp.exp(masked_scores(query_blk, key_blk, key_mask) - log_total)
    grad_probs = jnp.einsum(
        "bahd,bchd->bhac", grad_att_blk, value_blk, preferred_element_type=jnp.float32
    )
    grad_scores = (
        probs * (grad_probs - jnp.sum(grad_probs * probs, axis=-1, keepdims=True))
    ).astype(jnp.bfloat16)
    grad_query = jnp.einsum(
        "bhac,bchd->bahd", grad_scores, key_blk, preferred_element_type=jnp.float32
    ) * HEAD ** (-0.5)
    grad_query = grad_query.reshape(tok_rows, model_width).astype(jnp.bfloat16)
    key_parts = jnp.einsum(
        "bhac,bahd->bchd", grad_scores, query_blk, preferred_element_type=jnp.float32
    ) * HEAD ** (-0.5)
    grad_key = fold_keys(key_parts, tok_rows, model_width).astype(jnp.bfloat16)
    value_parts = jnp.einsum(
        "bhac,bahd->bchd", probs_low, grad_att_blk, preferred_element_type=jnp.float32
    )
    grad_value = fold_keys(value_parts, tok_rows, model_width).astype(jnp.bfloat16)
    grad_normed_one = (
        dot_back(grad_query, query_w) + dot_back(grad_key, key_w) + dot_back(grad_value, value_w)
    )
    grad_gain_one = jnp.sum(grad_normed_one * unit_one, axis=0)
    grad_dealt = (grad_middle + norm_back(grad_normed_one, gain_one, unit_one, inverse_one)).astype(
        jnp.bfloat16
    )
    returned_out, returned_grad = (
        lax.all_to_all(result, "dp", split_axis=0, concat_axis=0, tiled=True),
        lax.all_to_all(grad_dealt, "dp", split_axis=0, concat_axis=0, tiled=True),
    )
    layer_out = returned_out[send_slot]
    input_grad = returned_grad[send_slot]
    attn_entries = [
        ("gain", grad_gain_one),
        ("mat", normed_one, grad_query),
        ("mat", normed_one, grad_key),
        ("mat", normed_one, grad_value),
        ("mat", attended, grad_branch),
    ]
    every_entry = attn_entries + ff_entries
    all_summed = lax.psum_scatter(
        term_maker(every_entry, pieces, lax.axis_size(("dp", "fsdp")) * 1),
        ("dp", "fsdp"),
        scatter_dimension=0,
        tiled=True,
    )
    all_spans = split_spans(all_summed, every_entry, pieces)
    (
        span_gain_one,
        span_query,
        span_key,
        span_value,
        span_out,
        span_gain_two,
        span_gate,
        span_up,
        span_down,
    ) = all_spans
    return (
        layer_out,
        input_grad,
        span_gain_one,
        span_query,
        span_key,
        span_value,
        span_out,
        span_gain_two,
        span_gate,
        span_up,
        span_down,
    )


def solution(mesh):
    in_specs = (
        P(("dp", "fsdp"), None),
        P(("dp", "fsdp")),
        P(("dp", "fsdp"), None),
        P(("dp", "fsdp")),
        P(("dp", "fsdp")),
        P(("dp", "fsdp")),
        P(("dp", "fsdp")),
        P(("dp", "fsdp")),
        P(("dp", "fsdp")),
        P(("dp", "fsdp")),
        P(("dp", "fsdp")),
        P(("dp", "fsdp")),
        P(("dp", "fsdp"), None),
    )
    out_specs = (
        P(("dp", "fsdp"), None),
        P(("dp", "fsdp"), None),
        P(("dp", "fsdp")),
        P(("dp", "fsdp")),
        P(("dp", "fsdp")),
        P(("dp", "fsdp")),
        P(("dp", "fsdp")),
        P(("dp", "fsdp")),
        P(("dp", "fsdp")),
        P(("dp", "fsdp")),
        P(("dp", "fsdp")),
    )
    return jax.shard_map(body, mesh=mesh, in_specs=in_specs, out_specs=out_specs, check_vma=False)
```

profile of v0, /device:TPU:0, one launch (start us, length us, event | category | flops | bytes accessed | tf_op | source)
XLA Modules:
  0.0 1515.1 jit_solution(10308446540534388259)
XLA Ops:
  14.8 8.3 all-to-all-start
  25.5 41.0 %all-reduce.8 = (bf16[1024]{0:T(1024)(128)(2,1)S(1)}, bf16[1024]{0:T(1024)(128)(2,1)S(1)}) all-reduce(bf16[1024]{0:T(1024)(128)(2,1)S(1)} %dynamic-update-slice, bf16[1024]{0:T(1024)(128)(2,1)S(1)} %dynamic-update-slice.1), channel_id=1, replica_groups=mesh['dp'=16,'fsdp'=2] {'dp','fsdp'}, use_global_device_ids=true, to_apply=%add.5 | all-reduce | flops 2048 | bytes 8192
  69.0 5.6 all-to-all-start.2
  74.9 3.3 reshape.268
  80.8 47.9 %all-gather.12.cloned.1.call-done = bf16[1048576]{0:T(1024)(128)(2,1)} async-done(((bf16[32768]{0:T(1024)(128)(2,1)}), bf16[1048576]{0:T(1024)(128)(2,1)}) %all-gather.12.cloned.1.call-update) | async-done | bytes 2097168 | tf_op jit(solution)/shard_map/all_gather | solution.py:154
  128.7 4.2 reshape.274
  141.9 44.9 %all-gather.10.cloned.1.call-done = bf16[1048576]{0:T(1024)(128)(2,1)} async-done(((bf16[32768]{0:T(1024)(128)(2,1)}), bf16[1048576]{0:T(1024)(128)(2,1)}) %all-gather.10.cloned.1.call-update) | async-done | bytes 2097168 | tf_op jit(solution)/shard_map/all_gather | solution.py:153
  186.8 4.2 reshape.272
  201.7 3.1 fusion.5
  209.2 35.6 %all-gather.14.cloned.1.call-done = bf16[1048576]{0:T(1024)(128)(2,1)} async-done(((bf16[32768]{0:T(1024)(128)(2,1)}), bf16[1048576]{0:T(1024)(128)(2,1)}) %all-gather.14.cloned.1.call-update) | async-done | bytes 2097168 | tf_op jit(solution)/shard_map/all_gather | solution.py:156
  244.8 4.2 reshape.277
  252.9 60.1 %all-gather.16.cloned.1.call-done = bf16[2818048]{0:T(1024)(128)(2,1)} async-done(((bf16[88064]{0:T(1024)(128)(2,1)}), bf16[2818048]{0:T(1024)(128)(2,1)}) %all-gather.16.cloned.1.call-update) | async-done | bytes 5636112 | tf_op jit(solution)/shard_map/all_gather | solution.py:158
  313.0 10.8 reshape.278
  323.8 6.2 fusion.59
  330.0 51.3 %all-gather.18.cloned.1.call-done = bf16[2818048]{0:T(1024)(128)(2,1)} async-done(((bf16[88064]{0:T(1024)(128)(2,1)}), bf16[2818048]{0:T(1024)(128)(2,1)}) %all-gather.18.cloned.1.call-update) | async-done | bytes 5636112 | tf_op jit(solution)/shard_map/all_gather | solution.py:159
  381.3 11.0 reshape.279
  392.2 57.5 %all-gather.20.cloned.1.call-done = bf16[2818048]{0:T(1024)(128)(2,1)} async-done(((bf16[88064]{0:T(1024)(128)(2,1)}), bf16[2818048]{0:T(1024)(128)(2,1)}) %all-gather.20.cloned.1.call-update) | async-done | bytes 5636112 | tf_op jit(solution)/shard_map/all_gather | solution.py:160
  449.7 9.6 reshape.280
  459.3 6.2 fusion.60
  465.5 6.3 multiply_convert_fusion
  471.8 5.2 fusion.61
  477.0 4.9 multiply_reduce_fusion.1
  500.5 5.9 fusion.63
  506.4 5.9 fusion.64
  516.8 3.3 fusion.62
  535.6 5.0 reshape_reshape.29
  543.5 5.0 reshape_reshape.30
  551.4 4.9 reshape_reshape.31
  556.4 5.0 reshape_reshape.32
  561.4 12.0 reshape_reshape.33
  573.4 11.7 reshape_reshape.34
  585.1 6.7 fusion.26
  591.7 11.5 reshape_reshape.35
  604.6 14.8 dynamic-update-slice.3
  619.5 14.8 dynamic-update-slice.4
  634.3 14.8 dynamic-update-slice.5
  649.1 14.9 dynamic-update-slice.6
  665.5 31.6 %dynamic-update-slice.8 = f32[32,395328]{1,0:T(8,128)} dynamic-update-slice(f32[32,395328]{1,0:T(8,128)} %dynamic-update-slice.7, f32[32,88064]{1,0:T(8,128)} %reshape_reshape.33, s32[]{} %constant.107, s32[]{} %constant.113) | dynamic-update-slice | bytes 22544388
  697.1 31.6 %dynamic-update-slice.9 = f32[32,395328]{1,0:T(8,128)} dynamic-update-slice(f32[32,395328]{1,0:T(8,128)} %dynamic-update-slice.8, f32[32,88064]{1,0:T(8,128)} %reshape_reshape.34, s32[]{} %constant.107, s32[]{} %constant.114) | dynamic-update-slice | bytes 22544388
  728.7 31.5 %dynamic-update-slice.10 = f32[32,395328]{1,0:T(8,128)} dynamic-update-slice(f32[32,395328]{1,0:T(8,128)} %dynamic-update-slice.9, f32[32,88064]{1,0:T(8,128)} %reshape_reshape.35, s32[]{} %constant.107, s32[]{} %constant.115) | dynamic-update-slice | bytes 22544388 | tf_op jit(solution)/shard_map/concatenate | solution.py:67
  761.3 4.3 fusion.7
  765.7 4.6 all-to-all-start.1
  771.2 13.5 all-to-all-done.1
  784.7 3.7 all-to-all-start.3
  790.0 12.6 all-to-all-done.3
  804.2 691.9 %all-reduce.11.cloned.1.call-done = f32[32,395328]{1,0:T(8,128)} async-done(((f32[32,395328]{1,0:T(8,128)}), f32[32,395328]{1,0:T(8,128)}) %all-reduce.11.cloned.1.call-update) | async-done | bytes 50602000
  1497.3 6.7 fusion.56
  1504.0 4.1 fusion.57
  (144 shorter events, 96.0 us)
Async XLA Ops:
  7.2 67.7 %all-gather.8.cloned.1.call-start = ((), (), s32[]{:S(2)}) async-start(), calls=%async_computation.4 | async-start | bytes 2162688 | tf_op jit(solution)/shard_map/all_gather | solution.py:155
  7.9 120.8 %all-gather.12.cloned.1.call-start = ((), (), s32[]{:S(2)}) async-start(), calls=%async_computation.6 | async-start | bytes 2162688 | tf_op jit(solution)/shard_map/all_gather | solution.py:154
  8.7 178.2 %all-gather.10.cloned.1.call-start = ((), (), s32[]{:S(2)}) async-start(), calls=%async_computation.5 | async-start | bytes 2162688 | tf_op jit(solution)/shard_map/all_gather | solution.py:153
  9.4 235.4 %all-gather.14.cloned.1.call-start = ((), (), s32[]{:S(2)}) async-start(), calls=%async_computation.7 | async-start | bytes 2162688 | tf_op jit(solution)/shard_map/all_gather | solution.py:156
  10.0 303.0 %all-gather.16.cloned.1.call-start = ((), (), s32[]{:S(2)}) async-start(), calls=%async_computation.8 | async-start | bytes 5812224 | tf_op jit(solution)/shard_map/all_gather | solution.py:158
  10.6 370.7 %all-gather.18.cloned.1.call-start = ((), (), s32[]{:S(2)}) async-start(), calls=%async_computation.9 | async-start | bytes 5812224 | tf_op jit(solution)/shard_map/all_gather | solution.py:159
  11.1 438.6 %all-gather.20.cloned.1.call-start = ((), (), s32[]{:S(2)}) async-start(), calls=%async_computation.10 | async-start | bytes 5812224 | tf_op jit(solution)/shard_map/all_gather | solution.py:160
  14.8 54.2 %all-to-all-start = ((bf16[16,8,1024]{2,1,0:T(8,128)(2,1)}), bf16[16,8,1024]{2,1,0:T(8,128)(2,1)S(1)}, u32[]{:S(2)}, u32[]{:S(2)}) async-start(bf16[16,8,1024]{2,1,0:T(8,128)(2,1)} %bitcast), calls=%async_computation | async-start | bytes 524288 | tf_op jit(solution)/shard_map/all_to_all | solution.py:141
  69.0 396.5 %all-to-all-start.2 = ((bf16[16,8,1024]{2,1,0:T(8,128)(2,1)}), bf16[16,8,1024]{2,1,0:T(8,128)(2,1)}, u32[]{:S(2)}, u32[]{:S(2)}) async-start(bf16[16,8,1024]{2,1,0:T(8,128)(2,1)} %bitcast.9), calls=%async_computation.2 | async-start | bytes 524288 | tf_op jit(solution)/shard_map/all_to_all | solution.py:142
  74.6 1421.4 %all-reduce.11.cloned.1.call-start = ((), (), s32[]{:S(2)}) async-start(), calls=%async_computation.11 | async-start | bytes 101220352
  198.4 0.8 copy-start.11
  251.3 0.8 copy-start.1
  471.8 5.2 copy-start.16
  471.8 10.1 copy-start.14
  471.8 5.2 copy-start.2
  477.0 6.9 copy-start
  483.1 0.8 copy-start.4
  489.8 3.2 copy-start.10
  489.8 3.2 copy-start.12
  489.8 4.5 copy-start.9
  492.3 3.4 copy-start.20
  493.0 4.7 copy-start.5
  493.0 4.7 copy-start.18
  495.7 4.8 copy-start.7
  495.7 4.8 copy-start.17
  500.5 5.9 copy-start.15
  512.3 7.8 copy-start.8
  526.9 5.8 copy-start.19
  573.4 11.7 copy-start.13
  760.3 1.0 copy-start.3
  761.3 8.9 copy-start.6
  761.3 8.9 copy-start.21
  765.7 19.0 %all-to-all-start.1 = ((bf16[16,8,1024]{2,1,0:T(8,128)(2,1)}), bf16[16,8,1024]{2,1,0:T(8,128)(2,1)S(1)}, u32[]{:S(2)}, u32[]{:S(2)}) async-start(bf16[16,8,1024]{2,1,0:T(8,128)(2,1)} %fusion.7), calls=%async_computation.1 | async-start | bytes 524288 | tf_op jit(solution)/shard_map/all_to_all | solution.py:259
  784.7 17.9 %all-to-all-start.3 = ((bf16[16,8,1024]{2,1,0:T(8,128)(2,1)}), bf16[16,8,1024]{2,1,0:T(8,128)(2,1)S(1)}, u32[]{:S(2)}, u32[]{:S(2)}) async-start(bf16[16,8,1024]{2,1,0:T(8,128)(2,1)} %fusion.25), calls=%async_computation.3 | async-start | bytes 524288 | tf_op jit(solution)/shard_map/all_to_all | solution.py:260
Sparse Core Ops, SparseCore 0:
  10.9 59.5 all-gather.7
  73.4 55.2 all-gather.11
  131.6 55.2 all-gather.9
  189.5 55.2 all-gather.13
  247.5 65.4 all-gather.15
  315.7 65.5 all-gather.17
  384.1 65.5 all-gather.19
  760.4 735.5 all-reduce.10
where the time goes:
time: 1530 us; the launch traced here: 1520 us
  waiting for transfers between devices  1020 us (67%)
  local copies, waits for them, and re-layouts  317 us (21%)
  matrix products  91.2 us (6%)
  blocking collectives  41 us (3%)
  starting transfers between devices  22.5 us (1%)
  between operations  15.4 us (1%)
    unnamed x9, waiting for transfers between devices  696 us
    unnamed x56, local copies, waits for them, and re-layouts  131 us
    all_gather x1, waiting for transfers between devices, body(): lax.all_gather(flat_weights[6], ('dp', 'fsdp'), axis=0, tiled=True)  60.1 us
    all_gather x1, waiting for transfers between devices, body(): lax.all_gather(flat_weights[8], ('dp', 'fsdp'), axis=0, tiled=True)  57.5 us
    another operation x7, local copies, waits for them, and re-layouts, flat_piece(): return flat.reshape(count, share)  55 us
    all_gather x1, waiting for transfers between devices, body(): lax.all_gather(flat_weights[7], ('dp', 'fsdp'), axis=0, tiled=True)  51.3 us
    all_gather x1, waiting for transfers between devices, body(): lax.all_gather(flat_weights[2], ('dp', 'fsdp'), axis=0, tiled=True)  47.9 us
    all_gather x1, waiting for transfers between devices, body(): lax.all_gather(flat_weights[1], ('dp', 'fsdp'), axis=0, tiled=True)  44.9 us
  transfers between devices with their start and end apart: 12, of which 9 were waited for; matrix products, arithmetic and copies ran while one was open for 7% of the time, Pallas kernels for 0%

commit v1 on v0

--- a/solution.py
+++ b/solution.py
@@ -1,6 +1,11 @@
+import functools
+from types import SimpleNamespace
+
 import jax
 import jax.numpy as jnp
 from jax import lax
+from jax.experimental import pallas as pl
+from jax.experimental.pallas import tpu as pltpu
 from jax.sharding import PartitionSpec as P
 
 HEAD = 64
@@ -302,6 +307,864 @@
     )
 
 
+MESH = pl.DeviceIdType.MESH
+TP = 4
+CORES = 2
+PAD = 96
+VMEM_BYTES = 62 * 2**20
+
+QKV, GATE, UP, OUT, DOWN = range(5)
+F32 = jnp.float32
+BF16 = jnp.bfloat16
+
+
+def remote(src, dst, send, recv, device):
+    return pltpu.make_async_remote_copy(
+        src_ref=src, dst_ref=dst, send_sem=send, recv_sem=recv, device_id=device, device_id_type=MESH
+    )
+
+
+def nn(a, b):
+    return lax.dot_general(a, b, (((1,), (0,)), ((), ())), preferred_element_type=F32)
+
+
+def nt(a, b):
+    return lax.dot_general(a, b, (((1,), (1,)), ((), ())), preferred_element_type=F32)
+
+
+def tn(a, b):
+    return lax.dot_general(a, b, (((0,), (0,)), ((), ())), preferred_element_type=F32)
+
+
+def row_of(tile):
+    return jnp.concatenate([tile[k : k + 1] for k in range(tile.shape[0])], axis=1)
+
+
+def tile_of(row):
+    return jnp.concatenate(
+        [row[:, k * 128 : (k + 1) * 128] for k in range(row.shape[1] // 128)], axis=0
+    )
+
+
+def block_kernel(
+    sizes,
+    tok,
+    cot,
+    deal,
+    lens,
+    gains,
+    scol,
+    sout,
+    sdown,
+    lout,
+    igrad,
+    ocol,
+    oout,
+    odown,
+    ogain,
+    b,
+    s,
+):
+    nd, zn, rows, width, hw, fw = sizes
+    heads = hw // HEAD
+    toks = TP * rows
+    per = rows // nd
+    dp = lax.axis_index("dp")
+    f = lax.axis_index("fsdp")
+    other = 1 - f
+    z = dp // TP
+    c = dp % TP
+    sib = (dp, other)
+    row_dev = width // (nd * CORES)
+
+    barrier = pltpu.get_barrier_semaphore()
+    pl.semaphore_signal(barrier, inc=1, device_id=sib, device_id_type=MESH)
+
+    @pl.loop(1, nd)
+    def _(k):
+        pl.semaphore_signal(
+            barrier, inc=1, device_id=(lax.rem(dp + k, nd), f), device_id_type=MESH
+        )
+
+    def all_peers(src, dst, send, recv, start=True):
+        @pl.loop(1, nd)
+        def _(k):
+            to = lax.rem(dp + k, nd)
+            remote(src(to), dst.at[dp], send.at[k], recv.at[k], (to, f)).start()
+
+    def all_peers_recv(src, dst, send, recv):
+        @pl.loop(1, nd)
+        def _(k):
+            at = lax.rem(dp + (nd - k), nd)
+            remote(src(at), dst.at[at], send.at[k], recv.at[k], (at, f)).wait_recv()
+
+    def all_peers_sent(src, dst, send, recv):
+        @pl.loop(1, nd)
+        def _(k):
+            to = lax.rem(dp + k, nd)
+            remote(src(to), dst.at[dp], send.at[k], recv.at[k], (to, f)).wait_send()
+
+    def plane(k):
+        cc = lax.rem(c + k, TP)
+        return cc, (z * TP + cc, f)
+
+    def gather_start(buf, send, recv):
+        for k in range(1, TP):
+            _, dev = plane(k)
+            remote(buf.at[c], buf.at[c], send.at[k], recv.at[k], dev).start()
+
+    def gather_recv(buf, send, recv):
+        for k in range(1, TP):
+            cc, dev = plane(TP - k)
+            remote(buf.at[c], buf.at[cc], send.at[k], recv.at[k], dev).wait_recv()
+
+    def gather_sent(buf, send, recv):
+        for k in range(1, TP):
+            _, dev = plane(k)
+            remote(buf.at[c], buf.at[c], send.at[k], recv.at[k], dev).wait_send()
+
+    tiles = 4
+    tw = width // tiles
+
+    def part(buf, at, j):
+        return buf.at[at, :, pl.ds(pl.multiple_of(j * tw, tw), tw)]
+
+    def scatter_tile(src, dst, send, recv, j):
+        for k in range(1, TP):
+            cc, dev = plane(k)
+            remote(part(src, cc, j), part(dst, c, j), send.at[j, k], recv.at[j, k], dev).start()
+
+    def scatter_recv(src, dst, send, recv):
+        @pl.loop(0, tiles)
+        def _(j):
+            for k in range(1, TP):
+                cc, dev = plane(TP - k)
+                remote(
+                    part(src, cc, j), part(dst, cc, j), send.at[j, k], recv.at[j, k], dev
+                ).wait_recv()
+
+    def scatter_sent(src, dst, send, recv):
+        @pl.loop(0, tiles)
+        def _(j):
+            for k in range(1, TP):
+                cc, dev = plane(k)
+                remote(
+                    part(src, cc, j), part(dst, c, j), send.at[j, k], recv.at[j, k], dev
+                ).wait_send()
+
+    def scatter_sum(src, dst):
+        total = src[c].astype(F32)
+        for k in range(1, TP):
+            total = total + dst[lax.rem(c + k, TP)].astype(F32)
+        return total
+
+    def block(piece, at, core):
+        if piece == OUT:
+            return b.wout.at[at, core]
+        if piece == DOWN:
+            return b.wdown.at[at, core]
+        return b.wcol.at[piece, at, :, core]
+
+    def hop(piece, at, slot, to):
+        return remote(
+            block(piece, at, f),
+            block(piece, at, f),
+            s.z_s.at[piece, slot],
+            s.z_r.at[piece, at],
+            (to * TP + c, f),
+        )
+
+    def mirror(piece, at, core):
+        return remote(
+            block(piece, at, core),
+            block(piece, at, core),
+            s.b_s.at[piece, at],
+            s.b_r.at[piece, at],
+            sib,
+        )
+
+    def line_start(piece):
+        @pl.when(z < zn - 1)
+        def _():
+            hop(piece, z, 0, z + 1).start()
+
+        @pl.when(z > 0)
+        def _():
+            hop(piece, z, 1, z - 1).start()
+
+        mirror(piece, z, f).start()
+
+    def line_step(piece, d):
+        @pl.when(z >= d)
+        def _():
+            hop(piece, z - d, 0, z).wait_recv()
+
+            @pl.when(z < zn - 1)
+            def _():
+                hop(piece, z - d, 2 * d, z + 1).start()
+
+            mirror(piece, z - d, f).start()
+
+        @pl.when(z + d < zn)
+        def _():
+            hop(piece, z + d, 0, z).wait_recv()
+
+            @pl.when(z > 0)
+            def _():
+                hop(piece, z + d, 2 * d + 1, z - 1).start()
+
+            mirror(piece, z + d, f).start()
+
+    def line_done(piece):
+        for at in range(zn):
+            mirror(piece, at, other).wait_recv()
+
+    def line_sent(piece):
+        for d in range(zn):
+
+            @pl.when((z >= d) & (z < zn - 1))
+            def _():
+                hop(piece, z - d, 2 * d, z + 1).wait_send()
+
+            @pl.when((z + d < zn) & (z > 0))
+            def _():
+                hop(piece, z + d, 2 * d + 1, z - 1).wait_send()
+
+        for at in range(zn):
+            mirror(piece, at, f).wait_send()
+
+    def spread(piece, k):
+        cc, dev = plane(k)
+        return remote(
+            scol.at[piece, cc],
+            b.wcol.at[piece, z, c, f],
+            s.s1_s.at[piece, k],
+            s.s1_r.at[piece, k],
+            dev,
+        )
+
+    def spread_recv(piece):
+        for k in range(1, TP):
+            cc, dev = plane(TP - k)
+            remote(
+                scol.at[piece, cc],
+                b.wcol.at[piece, z, cc, f],
+                s.s1_s.at[piece, k],
+                s.s1_r.at[piece, k],
+                dev,
+            ).wait_recv()
+
+    slot = ((deal[...] >> _log2(rows * CORES)) * per) + (deal[...] & (per - 1))
+    pick = (lax.broadcasted_iota(jnp.int32, (rows, rows), 0) == slot).astype(BF16)
+    b.pick[...] = pick
+    b.tsend[...] = nn(pick, tok[...]).reshape(nd, per, width).astype(BF16)
+    b.csend[...] = nn(pick, cot[...]).reshape(nd, per, width).astype(BF16)
+
+    pl.semaphore_wait(barrier, nd)
+
+    all_peers(lambda to: gains, b.grecv, s.g_s, s.g_r)
+    all_peers(lambda to: b.tsend.at[to], b.trecv, s.t_s, s.t_r)
+    for k in range(1, TP):
+        spread(QKV, k).start()
+    for piece in (QKV, GATE, UP):
+        b.wcol[piece, z, c, f] = scol[piece, c]
+    b.wout[z, f] = sout[...]
+    b.wdown[z, f] = sdown[...]
+    b.trecv[dp] = b.tsend[dp]
+    b.crecv[dp] = b.csend[dp]
+    b.grecv[dp] = gains[...]
+    ri = lax.broadcasted_iota(jnp.int32, (rows, rows), 0)
+    ci = lax.broadcasted_iota(jnp.int32, (rows, rows), 1)
+    seg_r = jnp.zeros((rows, rows), jnp.int32)
+    seg_c = jnp.zeros((rows, rows), jnp.int32)
+    bound = jnp.int32(0)
+    for k in range(lens.shape[1]):
+        bound = bound + lens[0, k]
+        seg_r = seg_r + (ri >= bound).astype(jnp.int32)
+        seg_c = seg_c + (ci >= bound).astype(jnp.int32)
+    allowed = (seg_r == seg_c) & (ri >= ci) & (ri - ci < WINDOW)
+    b.mask[c] = allowed.astype(F32).astype(BF16)
+    gather_start(b.mask, s.m_s, s.m_r)
+    for piece in (GATE, UP):
+        for k in range(1, TP):
+            spread(piece, k).start()
+
+    all_peers_recv(lambda at: gains, b.grecv, s.g_s, s.g_r)
+    gain_sum = jnp.sum(b.grecv[...].astype(F32), axis=0)
+    b.gpart[f] = gain_sum.astype(BF16)
+    gmirror = remote(b.gpart.at[f], b.gpart.at[f], s.gb_s, s.gb_r, sib)
+    gmirror.start()
+
+    spread_recv(QKV)
+    line_start(QKV)
+
+    all_peers_recv(lambda at: b.tsend.at[at], b.trecv, s.t_s, s.t_r)
+    all_peers(lambda to: b.csend.at[to], b.crecv, s.c_s, s.c_r)
+    remote(b.gpart.at[other], b.gpart.at[other], s.gb_s, s.gb_r, sib).wait_recv()
+    gain_tile = b.gpart[0].astype(F32) + b.gpart[1].astype(F32)
+    gw = width // 128
+    b.gain[0:1] = row_of(gain_tile[0:gw])
+    b.gain[1:2] = row_of(gain_tile[gw : 2 * gw])
+
+    x = b.trecv[...].astype(F32).reshape(rows, width)
+    unit = x * lax.rsqrt(jnp.mean(x * x, axis=1, keepdims=True) + EPSILON)
+    b.n1[c] = (unit * b.gain[0:1]).astype(BF16)
+    gather_start(b.n1, s.a_s.at[0], s.a_r.at[0])
+
+    line_step(QKV, 1)
+    line_start(OUT)
+    line_step(QKV, 2)
+    line_step(QKV, 3)
+    spread_recv(GATE)
+    spread_recv(UP)
+    line_start(GATE)
+    line_step(OUT, 1)
+    all_peers_recv(lambda at: b.csend.at[at], b.crecv, s.c_s, s.c_r)
+    b.call[c] = b.crecv[...].reshape(rows, width)
+    gather_recv(b.n1, s.a_s.at[0], s.a_r.at[0])
+    gather_start(b.call, s.a_s.at[1], s.a_r.at[1])
+    line_done(QKV)
+    n1 = b.n1[...].reshape(toks, width)
+    for j in range(3):
+        w = b.wcol[QKV, :, :, :, :, j * hw : (j + 1) * hw].reshape(width, hw)
+        b.qkv[:, j * hw : (j + 1) * hw] = nn(n1, w).astype(BF16)
+    line_step(OUT, 2)
+    line_step(GATE, 1)
+    line_start(UP)
+    gather_recv(b.mask, s.m_s, s.m_r)
+    scale = HEAD ** (-0.5)
+
+    @pl.loop(0, TP)
+    def _(i):
+        at = pl.ds(pl.multiple_of(i * rows, rows), rows)
+        blk = b.qkv[at, :]
+        allow = b.mask[i].astype(F32) > 0.5
+        outs = []
+        for h in range(heads):
+            q = blk[:, h * HEAD : (h + 1) * HEAD]
+            k = blk[:, hw + h * HEAD : hw + (h + 1) * HEAD]
+            v = blk[:, 2 * hw + h * HEAD : 2 * hw + (h + 1) * HEAD]
+            scores = jnp.where(allow, nt(q, k) * scale, -1e30)
+            e = jnp.exp(scores - jnp.max(scores, axis=1, keepdims=True))
+            p = e / jnp.sum(e, axis=1, keepdims=True)
+            b.probs[i * heads + h] = p
+            outs.append(nn(p.astype(BF16), v))
+        b.att[at, :] = jnp.concatenate(outs, axis=1).astype(BF16)
+
+    line_step(OUT, 3)
+    line_step(GATE, 2)
+    line_step(UP, 1)
+    line_done(OUT)
+    att = b.att[...]
+
+    @pl.loop(0, tiles)
+    def _(j):
+        cols = pl.ds(pl.multiple_of(j * tw, tw), tw)
+        w = b.wout[:, :, :, cols].reshape(hw, tw)
+        b.p[0][:, :, cols] = nn(att, w).reshape(TP, rows, tw).astype(BF16)
+        scatter_tile(b.p[0], b.q[0], s.r_s.at[0], s.r_r.at[0], j)
+
+    line_step(GATE, 3)
+    line_start(DOWN)
+    line_step(UP, 2)
+    scatter_recv(b.p[0], b.q[0], s.r_s.at[0], s.r_r.at[0])
+    middle = b.trecv[...].astype(F32).reshape(rows, width) + scatter_sum(b.p[0], b.q[0])
+    b.middle[...] = middle
+    unit = middle * lax.rsqrt(jnp.mean(middle * middle, axis=1, keepdims=True) + EPSILON)
+    b.n2[c] = (unit * b.gain[1:2]).astype(BF16)
+    gather_start(b.n2, s.a_s.at[2], s.a_r.at[2])
+    line_step(UP, 3)
+    line_step(DOWN, 1)
+    line_done(GATE)
+    line_done(UP)
+    gather_recv(b.n2, s.a_s.at[2], s.a_r.at[2])
+    n2 = b.n2[...].reshape(toks, width)
+    fb = 256
+    for j in range(fw // fb):
+        cols = slice(j * fb, (j + 1) * fb)
+        gate = nn(n2, b.wcol[GATE, :, :, :, :, cols].reshape(width, fb))
+        up = nn(n2, b.wcol[UP, :, :, :, :, cols].reshape(width, fb))
+        b.gate[:, cols] = gate
+        b.up[:, cols] = up
+        b.hid[:, cols] = (gate * jax.nn.sigmoid(gate) * up).astype(BF16)
+    line_step(DOWN, 2)
+
+    gather_recv(b.call, s.a_s.at[1], s.a_r.at[1])
+    call = b.call[...].reshape(toks, width)
+
+    def presum(piece, src, dst):
+        return remote(src, dst, s.p_s.at[piece], s.p_r.at[piece], sib)
+
+    def row_send(piece, src, dst, start):
+        for k in range(1, zn):
+            zz = lax.rem(z + k, zn)
+            cp = remote(
+                src.at[zz], dst.at[z], s.w_s.at[piece, k], s.w_r.at[piece, k], (zz * TP + c, f)
+            )
+            cp.start() if start else cp.wait_send()
+
+    def row_recv(piece, src, dst):
+        for k in range(1, zn):
+            zz = lax.rem(z + (zn - k), zn)
+            remote(
+                src.at[zz], dst.at[zz], s.w_s.at[piece, k], s.w_r.at[piece, k], (zz * TP + c, f)
+            ).wait_recv()
+
+    for j in range(fw // (4 * PAD)):
+        w = tn(b.hid[:, j * 4 * PAD : (j + 1) * 4 * PAD], call)
+        b.gdown[2 * j : 2 * j + 2] = w.reshape(2, CORES, PAD, width).astype(BF16)
+    presum(DOWN, b.gdown.at[:, other], b.cdown).start()
+    line_step(DOWN, 3)
+    line_done(DOWN)
+    for j in range(fw // (4 * PAD)):
+        cols = slice(j * 4 * PAD, (j + 1) * 4 * PAD)
+        gh = nt(call, b.wdown[2 * j : 2 * j + 2].reshape(4 * PAD, width))
+        gate = b.gate[:, cols]
+        sg = jax.nn.sigmoid(gate)
+        b.ggate[:, cols] = (gh * b.up[:, cols] * sg * (1.0 + gate * (1.0 - sg))).astype(BF16)
+        b.gup[:, cols] = (gh * gate * sg).astype(BF16)
+
+    presum(DOWN, b.gdown.at[:, f], b.cdown).wait_recv()
+    for at in range(zn):
+        b.sdown[at] = (b.gdown[at, f].astype(F32) + b.cdown[at].astype(F32)).astype(BF16)
+    row_send(DOWN, b.sdown, b.rdown, True)
+    b.rdown[z] = b.sdown[z]
+
+    @pl.loop(0, tiles)
+    def _(j):
+        cols = pl.ds(pl.multiple_of(j * tw, tw), tw)
+        v = nt(b.ggate[...], b.wcol[GATE, j].reshape(tw, fw))
+        v = v + nt(b.gup[...], b.wcol[UP, j].reshape(tw, fw))
+        b.p[1][:, :, cols] = v.reshape(TP, rows, tw).astype(BF16)
+        scatter_tile(b.p[1], b.q[1], s.r_s.at[1], s.r_r.at[1], j)
+
+    def col_grad(piece, act, grad):
+        @pl.loop(0, zn)
+        def _(j):
+            a = act[:, :, pl.ds(pl.multiple_of(j * tw, tw), tw)].reshape(toks, tw)
+            g = tn(a, grad[...])
+            b.gcol[piece, j] = g.reshape(TP, CORES, row_dev, fw).astype(BF16)
+
+        presum(piece, b.gcol.at[piece, :, :, other], b.ccol.at[piece]).start()
+
+    def col_send(piece):
+        presum(piece, b.gcol.at[piece, :, :, f], b.ccol.at[piece]).wait_recv()
+
+        @pl.loop(0, zn)
+        def _(j):
+            v = b.gcol[piece, j, :, f].astype(F32) + b.ccol[piece, j].astype(F32)
+            b.scol[piece, j] = v.astype(BF16)
+
+        @pl.loop(1, nd)
+        def _(k):
+            to = lax.rem(dp + k, nd)
+            remote(
+                b.scol.at[piece, to // TP, to % TP],
+                b.rcol.at[piece, z, c],
+                s.w_s.at[piece, k],
+                s.w_r.at[piece, k],
+                (to, f),
+            ).start()
+
+        b.rcol[piece, z, c] = b.scol[piece, z, c]
+
+    def col_recv(piece):
+        @pl.loop(1, nd)
+        def _(k):
+            at = lax.rem(dp + (nd - k), nd)
+            remote(
+                b.scol.at[piece, z, c],
+                b.rcol.at[piece, at // TP, at % TP],
+                s.w_s.at[piece, k],
+                s.w_r.at[piece, k],
+                (at, f),
+            ).wait_recv()
+
+        total = b.rcol[piece, 0].astype(F32)
+        for k in range(1, zn):
+            total = total + b.rcol[piece, k].astype(F32)
+        ocol[piece] = total
+
+    def col_sent(piece):
+        @pl.loop(1, nd)
+        def _(k):
+            to = lax.rem(dp + k, nd)
+            remote(
+                b.scol.at[piece, to // TP, to % TP],
+                b.rcol.at[piece, z, c],
+                s.w_s.at[piece, k],
+                s.w_r.at[piece, k],
+                (to, f),
+            ).wait_send()
+
+    col_grad(GATE, b.n2, b.ggate)
+    col_grad(UP, b.n2, b.gup)
+    col_send(GATE)
+
+    scatter_recv(b.p[1], b.q[1], s.r_s.at[1], s.r_r.at[1])
+    gn = scatter_sum(b.p[1], b.q[1])
+    middle = b.middle[...]
+    inv = lax.rsqrt(jnp.mean(middle * middle, axis=1, keepdims=True) + EPSILON)
+    unit = middle * inv
+    b.ggain[1:2] = jnp.sum(gn * unit, axis=0, keepdims=True)
+    a = gn * b.gain[1:2]
+    gm = b.call[c].astype(F32) + inv * (a - unit * jnp.mean(a * unit, axis=1, keepdims=True))
+    b.gmid[...] = gm
+    b.gb[c] = gm.astype(BF16)
+    gather_start(b.gb, s.a_s.at[3], s.a_r.at[3])
+    col_send(UP)
+
+    hid = b.hid[...]
+
+    @pl.loop(0, tiles)
+    def _(j):
+        cols = pl.ds(pl.multiple_of(j * tw, tw), tw)
+        w = b.wdown[:, :, :, cols].reshape(fw, tw)
+        b.p[2][:, :, cols] = nn(hid, w).reshape(TP, rows, tw).astype(BF16)
+        scatter_tile(b.p[2], b.q[2], s.r_s.at[2], s.r_r.at[2], j)
+
+    gather_recv(b.gb, s.a_s.at[3], s.a_r.at[3])
+    gb = b.gb[...].reshape(toks, width)
+    b.ga[...] = nt(gb, b.wout[...].reshape(hw, width)).astype(BF16)
+    b.gout[...] = tn(b.att[...], gb).reshape(zn, CORES, row_dev, width).astype(BF16)
+    presum(OUT, b.gout.at[:, other], b.cout).start()
+
+    @pl.loop(0, TP)
+    def _(i):
+        at = pl.ds(pl.multiple_of(i * rows, rows), rows)
+        blk = b.qkv[at, :]
+        gab = b.ga[at, :]
+        gq, gk, gv = [], [], []
+        for h in range(heads):
+            q = blk[:, h * HEAD : (h + 1) * HEAD]
+            k = blk[:, hw + h * HEAD : hw + (h + 1) * HEAD]
+            v = blk[:, 2 * hw + h * HEAD : 2 * hw + (h + 1) * HEAD]
+            ga = gab[:, h * HEAD : (h + 1) * HEAD]
+            p = b.probs[i * heads + h]
+            gp = nt(ga, v)
+            gs = (p * (gp - jnp.sum(p * gp, axis=1, keepdims=True))).astype(BF16)
+            gq.append(nn(gs, k) * scale)
+            gk.append(tn(gs, q) * scale)
+            gv.append(tn(p.astype(BF16), ga))
+        b.gqkv[at, :] = jnp.concatenate(gq + gk + gv, axis=1).astype(BF16)
+
+    presum(OUT, b.gout.at[:, f], b.cout).wait_recv()
+    for at in range(zn):
+        b.sout[at] = (b.gout[at, f].astype(F32) + b.cout[at].astype(F32)).astype(BF16)
+    row_send(OUT, b.sout, b.rout, True)
+    b.rout[z] = b.sout[z]
+
+    @pl.loop(0, tiles)
+    def _(j):
+        cols = pl.ds(pl.multiple_of(j * tw, tw), tw)
+        v = nt(b.gqkv[...], b.wcol[QKV, j].reshape(tw, fw))
+        b.p[3][:, :, cols] = v.reshape(TP, rows, tw).astype(BF16)
+        scatter_tile(b.p[3], b.q[3], s.r_s.at[3], s.r_r.at[3], j)
+
+    col_grad(QKV, b.n1, b.gqkv)
+
+    scatter_recv(b.p[2], b.q[2], s.r_s.at[2], s.r_r.at[2])
+    res = b.middle[...] + scatter_sum(b.p[2], b.q[2])
+    b.lsend[...] = res.reshape(nd, per, width).astype(BF16)
+    col_send(QKV)
+    all_peers(lambda to: b.lsend.at[to], b.lrecv, s.l_s, s.l_r)
+    b.lrecv[dp] = b.lsend[dp]
+
+    scatter_recv(b.p[3], b.q[3], s.r_s.at[3], s.r_r.at[3])
+    gn = scatter_sum(b.p[3], b.q[3])
+    x = b.trecv[...].astype(F32).reshape(rows, width)
+    inv = lax.rsqrt(jnp.mean(x * x, axis=1, keepdims=True) + EPSILON)
+    unit = x * inv
+    b.ggain[0:1] = jnp.sum(gn * unit, axis=0, keepdims=True)
+    a = gn * b.gain[0:1]
+    gx = b.gmid[...] + inv * (a - unit * jnp.mean(a * unit, axis=1, keepdims=True))
+    b.isend[...] = gx.reshape(nd, per, width).astype(BF16)
+    all_peers(lambda to: b.isend.at[to], b.irecv, s.i_s, s.i_r)
+    b.irecv[dp] = b.isend[dp]
+    b.hsend[...] = jnp.concatenate([tile_of(b.ggain[0:1]), tile_of(b.ggain[1:2])], axis=0)
+    all_peers(lambda to: b.hsend, b.hrecv, s.h_s, s.h_r)
+    b.hrecv[dp] = b.hsend[...]
+
+    all_peers_recv(lambda at: b.lsend.at[at], b.lrecv, s.l_s, s.l_r)
+    pick = b.pick[...]
+    lout[...] = tn(pick, b.lrecv[...].reshape(rows, width)).astype(BF16)
+    row_recv(DOWN, b.sdown, b.rdown)
+    odown[...] = jnp.sum(b.rdown[...].astype(F32), axis=0)
+    col_recv(GATE)
+    col_recv(UP)
+    row_recv(OUT, b.sout, b.rout)
+    oout[...] = jnp.sum(b.rout[...].astype(F32), axis=0)
+    all_peers_recv(lambda at: b.hsend, b.hrecv, s.h_s, s.h_r)
+    b.hpart[f] = jnp.sum(b.hrecv[...], axis=0)
+    hmirror = remote(b.hpart.at[f], b.hpart.at[f], s.hb_s, s.hb_r, sib)
+    hmirror.start()
+    all_peers_recv(lambda at: b.isend.at[at], b.irecv, s.i_s, s.i_r)
+    igrad[...] = tn(pick, b.irecv[...].reshape(rows, width)).astype(BF16)
+    remote(b.hpart.at[other], b.hpart.at[other], s.hb_s, s.hb_r, sib).wait_recv()
+    ogain[...] = b.hpart[0] + b.hpart[1]
+    col_recv(QKV)
+
+    gmirror.wait_send()
+    hmirror.wait_send()
+    all_peers_sent(lambda to: gains, b.grecv, s.g_s, s.g_r)
+    all_peers_sent(lambda to: b.tsend.at[to], b.trecv, s.t_s, s.t_r)
+    all_peers_sent(lambda to: b.csend.at[to], b.crecv, s.c_s, s.c_r)
+    all_peers_sent(lambda to: b.lsend.at[to], b.lrecv, s.l_s, s.l_r)
+    all_peers_sent(lambda to: b.isend.at[to], b.irecv, s.i_s, s.i_r)
+    all_peers_sent(lambda to: b.hsend, b.hrecv, s.h_s, s.h_r)
+    gather_sent(b.mask, s.m_s, s.m_r)
+    for i, buf in enumerate((b.n1, b.call, b.n2, b.gb)):
+        gather_sent(buf, s.a_s.at[i], s.a_r.at[i])
+    for i in range(4):
+        scatter_sent(b.p[i], b.q[i], s.r_s.at[i], s.r_r.at[i])
+    for piece in (QKV, GATE, UP):
+        for k in range(1, TP):
+            spread(piece, k).wait_send()
+        presum(piece, b.gcol.at[piece, :, :, other], b.ccol.at[piece]).wait_send()
+        col_sent(piece)
+    presum(OUT, b.gout.at[:, other], b.cout).wait_send()
+    presum(DOWN, b.gdown.at[:, other], b.cdown).wait_send()
+    row_send(OUT, b.sout, b.rout, False)
+    row_send(DOWN, b.sdown, b.rdown, False)
+    for piece in (QKV, GATE, UP, OUT, DOWN):
+        line_sent(piece)
+
+
+def _log2(n):
+    return n.bit_length() - 1
+
+
+def kernel_takes(dp_count, core_count, rows, width, hidden):
+    pieces = dp_count * core_count
+    zn = dp_count // TP
+    return (
+        core_count == CORES
+        and dp_count % TP == 0
+        and rows == 128
+        and rows % dp_count == 0
+        and rows // dp_count == 8
+        and width == zn * 256
+        and width // HEAD == dp_count
+        and width // pieces == HEAD // CORES
+        and hidden % pieces == 0
+        and hidden // pieces <= PAD
+        and PAD * CORES * zn % 256 == 0
+        and zn == 4
+    )
+
+
+def planned(
+    dp_count,
+    tokens,
+    dealing,
+    lengths,
+    norm1_gain,
+    w_query,
+    w_key,
+    w_value,
+    w_out,
+    norm2_gain,
+    w_gate,
+    w_up,
+    w_down,
+    cotangent,
+):
+    nd = dp_count
+    zn = nd // TP
+    rows, width = tokens.shape
+    pieces = nd * CORES
+    row_dev = width // pieces
+    hidden = w_gate.shape[0] * pieces // width
+    unit = hidden // pieces
+    hw = width // TP
+    fw = PAD * CORES * zn
+    me = lax.axis_index(("dp", "fsdp"))
+
+    def head_cols(w):
+        w = w.reshape(row_dev, zn, TP, HEAD)
+        return w.transpose(2, 0, 1, 3).reshape(TP, row_dev, hw)
+
+    def hidden_cols(w):
+        w = w.reshape(row_dev, zn, TP, CORES, unit)
+        w = jnp.pad(w, ((0, 0), (0, 0), (0, 0), (0, 0), (0, PAD - unit)))
+        return w.transpose(2, 0, 1, 3, 4).reshape(TP, row_dev, fw)
+
+    scol = jnp.stack(
+        [
+            jnp.concatenate([head_cols(w_query), head_cols(w_key), head_cols(w_value)], axis=2),
+            hidden_cols(w_gate),
+            hidden_cols(w_up),
+        ]
+    )
+    sout = w_out.reshape(row_dev, width)
+    sdown = jnp.pad(w_down.reshape(unit, width), ((0, PAD - unit), (0, 0)))
+    gw = width // 128
+    lanes = jnp.arange(128)[None, :]
+    tile_rows = jnp.arange(gw)[:, None]
+    mine = (tile_rows == me * row_dev // 128) & (lanes // row_dev == me % (128 // row_dev))
+
+    def gain_tile(gain):
+        return jnp.where(mine, jnp.tile(gain, 128 // row_dev)[None, :], 0).astype(BF16)
+
+    gains = jnp.concatenate([gain_tile(norm1_gain), gain_tile(norm2_gain)], axis=0)
+
+    toks = TP * rows
+    per = rows // nd
+    V = pltpu.VMEM
+    bufs = dict(
+        pick=V((rows, rows), BF16),
+        tsend=V((nd, per, width), BF16),
+        trecv=V((nd, per, width), BF16),
+        csend=V((nd, per, width), BF16),
+        crecv=V((nd, per, width), BF16),
+        lsend=V((nd, per, width), BF16),
+        lrecv=V((nd, per, width), BF16),
+        isend=V((nd, per, width), BF16),
+        irecv=V((nd, per, width), BF16),
+        grecv=V((nd, 2 * gw, 128), BF16),
+        gpart=V((CORES, 2 * gw, 128), BF16),
+        gain=V((8, width), F32),
+        ggain=V((8, width), F32),
+        hsend=V((2 * gw, 128), F32),
+        hrecv=V((nd, 2 * gw, 128), F32),
+        hpart=V((CORES, 2 * gw, 128), F32),
+        mask=V((TP, rows, rows), BF16),
+        wcol=V((3, zn, TP, CORES, row_dev, fw), BF16),
+        wout=V((zn, CORES, row_dev, width), BF16),
+        wdown=V((zn, CORES, PAD, width), BF16),
+        n1=V((TP, rows, width), BF16),
+        n2=V((TP, rows, width), BF16),
+        call=V((TP, rows, width), BF16),
+        gb=V((TP, rows, width), BF16),
+        qkv=V((toks, 3 * hw), BF16),
+        probs=V((TP * hw // HEAD, rows, rows), F32),
+        att=V((toks, hw), BF16),
+        middle=V((rows, width), F32),
+        gmid=V((rows, width), F32),
+        gate=V((toks, fw), F32),
+        up=V((toks, fw), F32),
+        hid=V((toks, fw), BF16),
+        ggate=V((toks, fw), BF16),
+        gup=V((toks, fw), BF16),
+        ga=V((toks, hw), BF16),
+        gqkv=V((toks, 3 * hw), BF16),
+        gcol=V((3, zn, TP, CORES, row_dev, fw), BF16),
+        ccol=V((3, zn, TP, row_dev, fw), BF16),
+        scol=V((3, zn, TP, row_dev, fw), BF16),
+        rcol=V((3, zn, TP, row_dev, fw), BF16),
+        gout=V((zn, CORES, row_dev, width), BF16),
+        cout=V((zn, row_dev, width), BF16),
+        sout=V((zn, row_dev, width), BF16),
+        rout=V((zn, row_dev, width), BF16),
+        gdown=V((zn, CORES, PAD, width), BF16),
+        cdown=V((zn, PAD, width), BF16),
+        sdown=V((zn, PAD, width), BF16),
+        rdown=V((zn, PAD, width), BF16),
+    )
+    bufs.update(
+        p=[V((TP, rows, width), BF16) for _ in range(4)],
+        q=[V((TP, rows, width), BF16) for _ in range(4)],
+    )
+    S = pltpu.SemaphoreType.DMA
+    each = S((nd,))
+    sems = dict(
+        g_s=each,
+        g_r=each,
+        t_s=each,
+        t_r=each,
+        c_s=each,
+        c_r=each,
+        l_s=each,
+        l_r=each,
+        i_s=each,
+        i_r=each,
+        h_s=each,
+        h_r=each,
+        gb_s=S(()),
+        gb_r=S(()),
+        hb_s=S(()),
+        hb_r=S(()),
+        m_s=S((TP,)),
+        m_r=S((TP,)),
+        s1_s=S((3, TP)),
+        s1_r=S((3, TP)),
+        z_s=S((5, 2 * zn)),
+        z_r=S((5, zn)),
+        b_s=S((5, zn)),
+        b_r=S((5, zn)),
+        a_s=S((4, TP)),
+        a_r=S((4, TP)),
+        r_s=S((4, 4, TP)),
+        r_r=S((4, 4, TP)),
+        p_s=S((5,)),
+        p_r=S((5,)),
+        w_s=S((5, nd)),
+        w_r=S((5, nd)),
+    )
+    n_io = 8 + 6
+    spaces, shape_of = jax.tree.flatten((bufs, sems))
+
+    def entry(*refs):
+        io, rest = refs[:n_io], refs[n_io:]
+        b, s = jax.tree.unflatten(shape_of, rest)
+        block_kernel((nd, zn, rows, width, hw, fw), *io, SimpleNamespace(**b), SimpleNamespace(**s))
+
+    vm = pl.BlockSpec(memory_space=pltpu.VMEM)
+    sm = pl.BlockSpec(memory_space=pltpu.SMEM)
+    lout, igrad, ocol, oout, odown, ogain = pl.pallas_call(
+        entry,
+        out_shape=(
+            jax.ShapeDtypeStruct((rows, width), BF16),
+            jax.ShapeDtypeStruct((rows, width), BF16),
+            jax.ShapeDtypeStruct((3, TP, row_dev, fw), F32),
+            jax.ShapeDtypeStruct((row_dev, width), F32),
+            jax.ShapeDtypeStruct((PAD, width), F32),
+            jax.ShapeDtypeStruct((2 * gw, 128), F32),
+        ),
+        in_specs=[vm, vm, vm, sm, vm, vm, vm, vm],
+        out_specs=(vm,) * 6,
+        scratch_shapes=spaces,
+        compiler_params=pltpu.CompilerParams(
+            collective_id=0, has_side_effects=True, vmem_limit_bytes=VMEM_BYTES
+        ),
+        name="block_fwd_bwd",
+    )(tokens, cotangent, dealing.reshape(1, rows), lengths, gains, scol, sout, sdown)
+
+    def head_rows(g):
+        g = g.reshape(TP, row_dev, zn, HEAD)
+        return g.transpose(1, 2, 0, 3).reshape(-1)
+
+    def hidden_rows(g):
+        g = g.reshape(TP, row_dev, zn, CORES, PAD)[..., :unit]
+        return g.transpose(1, 2, 0, 3, 4).reshape(-1)
+
+    def my_gain(tile):
+        return lax.dynamic_slice(tile.reshape(-1), (me * row_dev,), (row_dev,))
+
+    return (
+        lout,
+        igrad,
+        my_gain(ogain[:gw]),
+        head_rows(ocol[0, :, :, :hw]),
+        head_rows(ocol[0, :, :, hw : 2 * hw]),
+        head_rows(ocol[0, :, :, 2 * hw :]),
+        oout.reshape(-1),
+        my_gain(ogain[gw:]),
+        hidden_rows(ocol[1]),
+        hidden_rows(ocol[2]),
+        odown[:unit].reshape(-1),
+    )
+
+
+def dispatch(dp_count, core_count, *args):
+    tokens, w_gate = args[0], args[9]
+    rows, width = tokens.shape
+    hidden = w_gate.shape[0] * dp_count * core_count // width
+    if kernel_takes(dp_count, core_count, rows, width, hidden):
+        return planned(dp_count, *args)
+    return body(*args)
+
+
 def solution(mesh):
     in_specs = (
         P(("dp", "fsdp"), None),
@@ -331,4 +1194,6 @@
         P(("dp", "fsdp")),
         P(("dp", "fsdp")),
     )
-    return jax.shard_map(body, mesh=mesh, in_specs=in_specs, out_specs=out_specs, check_vma=False)
+    return jax.shard_map(
+        functools.partial(dispatch, mesh.shape["dp"], mesh.shape["fsdp"]),
+         mesh=mesh, in_specs=in_specs, out_specs=out_specs, check_vma=False)

time: 1530 us -> 207 us (0.14)
  waiting for transfers between devices: 1020 us -> 0 us
  local copies, waits for them, and re-layouts: 317 us -> 24.6 us
  Pallas kernels: 0 us -> 179 us
  matrix products: 91.2 us -> 0 us
  blocking collectives: 41 us -> 0 us
  starting transfers between devices: 22.5 us -> 0 us
    unnamed x9 -> x0, waiting for transfers between devices: 696 us -> none
    all_gather x7 -> x0, waiting for transfers between devices: 297 us -> none  [the longest x1 60.1 us: body(): lax.all_gather(flat_weights[6], ('dp', 'fsdp'), axis=0, tiled=True)]
    pallas_call x0 -> x1, Pallas kernels: none -> 179 us  [planned(): pl.pallas_call(entry, out_shape=(jax.ShapeDtypeStruct((rows, width), BF16...]
    unnamed x56 -> x17, local copies, waits for them, and re-layouts: 131 us -> 3.02 us
    dot_general x27 -> x0, matrix products: 91.2 us -> none  [the longest x7 30.1 us: dot_rows(): lax.dot_general(first_op, second_op, (((0,), (0,)), ((), ())), preferred_...]
    another operation x11 -> x12, local copies, waits for them, and re-layouts: 60 us -> 4.02 us  [the longest x2 1.32 us: gain_tile(): jnp.tile(gain, 128 // row_dev)[None, :]]
    reshape x18 -> x17, local copies, waits for them, and re-layouts: 58.9 us -> 12.8 us  [the longest x2 2.98 us: hidden_rows(): return g.transpose(1, 2, 0, 3, 4).reshape(-1)]
    unnamed x1 -> x0, blocking collectives: 41 us -> none
  transfers between devices with their start and end apart: 12 -> 0, of which waited for: 9 -> 0; matrix products, arithmetic and copies ran while one was open for 7% -> 0% of each run, Pallas kernels for 0% -> 0%
where the time goes in v1:
time: 207 us
  Pallas kernels  179 us (86%)
  local copies, waits for them, and re-layouts  24.6 us (12%)
    pallas_call x1, Pallas kernels, planned(): pl.pallas_call(entry, out_shape=(jax.ShapeDtypeStruct((rows, width), BF16...  179 us

profile of v1, /device:TPU:0, one launch (start us, length us, event | category | flops | bytes accessed | tf_op | source)
XLA Modules:
  0.0 206.9 jit_solution(11273016523728468002)
XLA Ops:
  1.4 0.7 tile.4
  2.0 0.1 broadcast_in_dim.24
  2.1 0.7 tile.5
  2.8 0.1 broadcast_in_dim.27
  2.9 0.1 and_select_fusion.1
  2.9 0.6 pad_maximum_fusion.1.refs_4_
  3.5 1.5 reshape.139.refs_6_
  5.0 1.0 reshape.131
  6.1 0.1 reshape.132
  6.3 1.0 reshape.133
  7.3 0.1 reshape.134
  7.5 0.1 reshape.135
  7.6 0.1 reshape.136
  7.8 0.1 reshape.140
  7.9 0.7 pad.13.refs_7_
  8.6 0.9 reshape.137
  9.5 0.3 pad_bitcast_fusion.1
  9.8 0.2 copy.27
  10.0 0.2 stack_reshape.6
  10.2 0.9 reshape.138
  11.1 0.3 pad_bitcast_fusion
  11.4 0.2 copy.28
  11.6 0.2 stack_reshape.7
  11.8 0.9 pad_maximum_fusion.refs_5_
  12.7 179.0 %block_fwd_bwd.1 = (bf16[128,1024]{1,0:T(8,128)(2,1)}, bf16[128,1024]{1,0:T(8,128)(2,1)}, f32[3,4,32,768]{3,2,1,0:T(8,128)}, f32[32,1024]{1,0:T(8,128)}, f32[96,1024]{1,0:T(8,128)}, /*index=5*/f32[16,128]{1,0:T(8,128)}) custom-call(bf16[128,1024]{1,0:T(8,128)(2,1)} %refs_0_.1, bf16[128,1024]{1,0:T(8,128)(2,1)} %refs_1_.1, s32[1,128]{1,0:T(1,128)} %bitcast.47, ...), custom_call_target="tpu_custom_call" | custom-call | tf_op jit(solution)/shard_map/block_fwd_bwd/pallas_call | solution.py:1114
  191.7 0.8 slice_bitcast_fusion
  192.5 0.6 dynamic_slice.7
  193.1 0.6 dynamic_slice.6
  193.6 1.6 copy.36
  195.2 1.0 slice.39
  196.2 0.8 reshape.149
  197.1 0.2 reshape_squeeze.17
  197.3 0.2 copy.42
  197.5 0.8 reshape.144
  198.3 0.7 reshape_squeeze.19
  198.9 0.3 copy_bitcast_fusion
  199.2 1.5 reshape.148
  200.7 0.2 reshape_squeeze.16
  200.9 0.2 copy.43
  201.1 0.8 reshape.143
  201.9 0.2 reshape_squeeze.15
  202.0 0.2 copy.44
  202.2 0.8 reshape.142
  203.0 0.7 reshape_squeeze.18
  203.7 0.3 copy_bitcast_fusion.1
  204.0 1.5 reshape.147
  205.5 0.7 copy.48
  206.2 0.7 copy.49
  (22 shorter events, 0.3 us)
Async XLA Ops:
  0.6 6.8 %copy-start.6 = (bf16[32768]{0:T(1024)(128)(2,1)S(1)}, bf16[32768]{0:T(1024)(128)(2,1)}, u32[]{:S(2)}) copy-start(bf16[32768]{0:T(1024)(128)(2,1)} %param.19) | copy-start | bytes 196612
  5.0 2.7 %copy-start.3 = (bf16[88064]{0:T(1024)(128)(2,1)S(1)}, bf16[88064]{0:T(1024)(128)(2,1)}, u32[]{:S(2)}) copy-start(bf16[88064]{0:T(1024)(128)(2,1)} %param.24) | copy-start | bytes 528388
  6.2 2.4 %copy-start.4 = (bf16[88064]{0:T(1024)(128)(2,1)S(1)}, bf16[88064]{0:T(1024)(128)(2,1)}, u32[]{:S(2)}) copy-start(bf16[88064]{0:T(1024)(128)(2,1)} %param.22) | copy-start | bytes 528388
  7.9 2.3 %copy-start.5 = (bf16[88064]{0:T(1024)(128)(2,1)S(1)}, bf16[88064]{0:T(1024)(128)(2,1)}, u32[]{:S(2)}) copy-start(bf16[88064]{0:T(1024)(128)(2,1)} %param.23) | copy-start | bytes 528388
  191.7 5.3 %copy-start = (f32[3,4,32,768]{3,2,1,0:T(8,128)S(1)}, f32[3,4,32,768]{3,2,1,0:T(8,128)}, u32[]{:S(2)}) copy-start(f32[3,4,32,768]{3,2,1,0:T(8,128)} %get-tuple-element.20) | copy-start | bytes 3538948
  203.7 1.8 copy-start.2
  203.7 2.5 %copy-start.1 = (bf16[128,1024]{1,0:T(8,128)(2,1)S(1)}, bf16[128,1024]{1,0:T(8,128)(2,1)}, u32[]{:S(2)}) copy-start(bf16[128,1024]{1,0:T(8,128)(2,1)} %get-tuple-element.44) | copy-start | bytes 786436

commit v2 on v1

--- a/solution.py
+++ b/solution.py
@@ -352,20 +352,32 @@
     cot,
     deal,
     lens,
-    gains,
-    scol,
-    sout,
-    sdown,
+    gain1,
+    gain2,
+    wq,
+    wk,
+    wv,
+    wo,
+    wg,
+    wu,
+    wd,
     lout,
     igrad,
-    ocol,
-    oout,
-    odown,
-    ogain,
+    ogain1,
+    oq,
+    ok,
+    ov,
+    oo,
+    ogain2,
+    og,
+    ou,
+    od,
     b,
     s,
 ):
-    nd, zn, rows, width, hw, fw = sizes
+    nd, zn, rows, width, hw, fw, share = sizes
+    scol = b.own
+    gains = b.gown
     heads = hw // HEAD
     toks = TP * rows
     per = rows // nd
@@ -386,6 +398,99 @@
             barrier, inc=1, device_id=(lax.rem(dp + k, nd), f), device_id_type=MESH
         )
 
+    me = dp * CORES + f
+    chunks = share * CORES * TP * zn // 64
+    lane = lax.broadcasted_iota(jnp.int32, (1, 128), 1)
+
+    def turned(v, by):
+        return pltpu.roll(v, by % 128, 1) if by % 128 else v
+
+    def heads_in(w, t):
+        n = w.shape[0]
+        b.flat[:n] = w[...].astype(F32)
+        per_row = width // 128
+        cols = [b.flat[pl.ds(j, row_dev, stride=per_row), :] for j in range(per_row)]
+        for cc in range(TP):
+            for u in range(hw // 128):
+                left, right = cols[4 * u + cc // 2], cols[4 * u + 2 + cc // 2]
+                tile = jnp.where(
+                    lane < HEAD, turned(left, HEAD * (cc % 2)), turned(right, HEAD * (1 - cc % 2))
+                )
+                at = t * hw + u * 128
+                scol[QKV, cc, :, at : at + 128] = tile.astype(BF16)
+
+    def heads_out(o, t):
+        per_row = width // 128
+        for j in range(per_row):
+            cc, h = 2 * (j % 2), j // 2
+            at = t * hw + (h // 2) * 128
+            left = b.rcol[QKV, cc, :, at : at + 128].astype(F32)
+            right = b.rcol[QKV, cc + 1, :, at : at + 128].astype(F32)
+            tile = jnp.where(
+                lane < HEAD, turned(left, HEAD * (h % 2)), turned(right, HEAD * (1 - h % 2))
+            )
+            o[pl.ds(j, row_dev, stride=per_row), :] = tile
+
+    def spans(cc, odd):
+        total = share * CORES * TP * zn
+        for k in range(CORES * zn):
+            src = total * odd + share * (CORES * TP * (k // CORES) + CORES * cc + k % CORES)
+            dst, left = PAD * k, share
+            while left:
+                n = min(left, 128 - src % 128, 128 - dst % 128)
+                yield src, dst, n
+                src, dst, left = src + n, dst + n, left - n
+
+    def hidden_in(w, piece):
+        n = w.shape[0]
+        b.flat[:n] = w[...].astype(F32)
+        for cc in range(TP):
+            for odd in range(2):
+                tiles_of = [jnp.zeros((row_dev // 2, 128), F32) for _ in range(fw // 128)]
+                for src, dst, ln in spans(cc, odd):
+                    v = b.flat[pl.ds(src // 128, row_dev // 2, stride=chunks), :]
+                    at = dst % 128
+                    keep = (lane >= at) & (lane < at + ln)
+                    tiles_of[dst // 128] = jnp.where(
+                        keep, turned(v, dst - src), tiles_of[dst // 128]
+                    )
+                for u, v in enumerate(tiles_of):
+                    b.pairs[u, pl.ds(odd, row_dev // 2, stride=2), :] = v
+            for u in range(fw // 128):
+                scol[piece, cc, :, u * 128 : (u + 1) * 128] = b.pairs[u].astype(BF16)
+
+    def hidden_out(o, piece):
+        todo = [[] for _ in range(chunks)]
+        for cc in range(TP):
+            for u in range(fw // 128):
+                b.wide[cc, u] = b.rcol[piece, cc, :, u * 128 : (u + 1) * 128].astype(F32)
+            for odd in range(2):
+                for src, dst, ln in spans(cc, odd):
+                    todo[src // 128].append((src, dst, ln, cc, odd))
+        for j in range(chunks):
+            tile = jnp.zeros((row_dev // 2, 128), F32)
+            for src, dst, ln, cc, odd in todo[j]:
+                v = b.wide[cc, dst // 128, pl.ds(odd, row_dev // 2, stride=2), :]
+                at = src % 128
+                keep = (lane >= at) & (lane < at + ln)
+                tile = jnp.where(keep, turned(v, src - dst), tile)
+            o[pl.ds(j, row_dev // 2, stride=chunks), :] = tile
+
+    def rows_in(w, out, n):
+        count = w.shape[0]
+        per_row = width // 128
+        b.flat[:count] = w[...].astype(F32)
+        if count < n * per_row:
+            b.flat[count : n * per_row] = jnp.zeros((n * per_row - count, 128), F32)
+        for j in range(per_row):
+            out[:, j * 128 : (j + 1) * 128] = b.flat[pl.ds(j, n, stride=per_row), :].astype(BF16)
+
+    def rows_out(o, v):
+        per_row = width // 128
+        n = o.shape[0] // per_row
+        for j in range(per_row):
+            o[pl.ds(j, n, stride=per_row), :] = v[:n, j * 128 : (j + 1) * 128]
+
     def all_peers(src, dst, send, recv, start=True):
         @pl.loop(1, nd)
         def _(k):
@@ -404,8 +509,13 @@
             to = lax.rem(dp + k, nd)
             remote(src(to), dst.at[dp], send.at[k], recv.at[k], (to, f)).wait_send()
 
+    cx = c % 2
+    cy = c // 2
+
     def plane(k):
-        cc = lax.rem(c + k, TP)
+        xx = 1 - cx if k % 2 else cx
+        yy = 1 - cy if k // 2 else cy
+        cc = yy * 2 + xx
         return cc, (z * TP + cc, f)
 
     def gather_start(buf, send, recv):
@@ -415,7 +525,7 @@
 
     def gather_recv(buf, send, recv):
         for k in range(1, TP):
-            cc, dev = plane(TP - k)
+            cc, dev = plane(k)
             remote(buf.at[c], buf.at[cc], send.at[k], recv.at[k], dev).wait_recv()
 
     def gather_sent(buf, send, recv):
@@ -426,41 +536,78 @@
     tiles = 4
     tw = width // tiles
 
-    def part(buf, at, j):
-        return buf.at[at, :, pl.ds(pl.multiple_of(j * tw, tw), tw)]
-
-    def scatter_tile(src, dst, send, recv, j):
-        for k in range(1, TP):
-            cc, dev = plane(k)
-            remote(part(src, cc, j), part(dst, c, j), send.at[j, k], recv.at[j, k], dev).start()
-
-    def scatter_recv(src, dst, send, recv):
-        @pl.loop(0, tiles)
-        def _(j):
-            for k in range(1, TP):
-                cc, dev = plane(TP - k)
-                remote(
-                    part(src, cc, j), part(dst, cc, j), send.at[j, k], recv.at[j, k], dev
-                ).wait_recv()
-
-    def scatter_sent(src, dst, send, recv):
-        @pl.loop(0, tiles)
-        def _(j):
-            for k in range(1, TP):
-                cc, dev = plane(k)
-                remote(
-                    part(src, cc, j), part(dst, c, j), send.at[j, k], recv.at[j, k], dev
-                ).wait_send()
-
-    def scatter_sum(src, dst):
+    def gather_one(buf, k, send, recv):
+        cc, dev = plane(k)
+        remote(buf.at[c], buf.at[cc], send.at[k], recv.at[k], dev).wait_recv()
+
+    def swap(src, dst, send, recv, k):
+        cc, dev = plane(k)
+        return remote(src.at[cc], dst.at[c], send.at[k], recv.at[k], dev)
+
+    def swap_recv(src, dst, send, recv, k):
+        cc, dev = plane(k)
+        remote(src.at[cc], dst.at[cc], send.at[k], recv.at[k], dev).wait_recv()
+
+    half = rows // 2
+    low, high = pl.ds(0, half), pl.ds(half, half)
+
+    def relay(buf, send, recv, k):
+        at = (plane(2)[0], c, c, plane(1)[0])[k]
+        ref = (buf.at[at, high], buf.at[at], buf.at[at], buf.at[at, low])[k]
+        return remote(ref, ref, send.at[k], recv.at[k], plane((1, 1, 2, 2)[k])[1])
+
+    def relay_wait(buf, send, recv, k):
+        at = plane((3, 1, 2, 3)[k])[0]
+        ref = (buf.at[at, high], buf.at[at], buf.at[at], buf.at[at, low])[k]
+        remote(ref, ref, send.at[k], recv.at[k], plane((1, 1, 2, 2)[k])[1]).wait_recv()
+
+    def relay_start(buf, send, recv):
+        relay(buf, send, recv, 1).start()
+        relay(buf, send, recv, 2).start()
+
+    def relay_pass(buf, send, recv):
+        relay_wait(buf, send, recv, 1)
+        relay(buf, send, recv, 3).start()
+        relay_wait(buf, send, recv, 2)
+        relay(buf, send, recv, 0).start()
+
+    def relay_done(buf, send, recv):
+        relay_wait(buf, send, recv, 3)
+        relay_wait(buf, send, recv, 0)
+
+    def halves(src, land, send, recv, k):
+        at = plane(3)[0]
+        part = src.at[at, low] if k else src.at[at, high]
+        return remote(part, land.at[k // 3], send.at[k], recv.at[k], plane(1 if k else 2)[1])
+
+    def side(src, dst, send, recv, k):
+        cc, dev = plane(k)
+        return remote(src.at[cc], dst.at[k - 1], send.at[k], recv.at[k], dev)
+
+    def reduce_start(src, land, send, recv):
+        halves(src, land, send, recv, 3).start()
+        halves(src, land, send, recv, 0).start()
+
+    def reduce_side(src, dst, land, send, recv, k):
+        cc = plane(k)[0]
+        if k == 1:
+            halves(src, land, send, recv, 0).wait_recv()
+            src[cc, half:] = (src[cc, half:].astype(F32) + land[0].astype(F32)).astype(BF16)
+        else:
+            halves(src, land, send, recv, 3).wait_recv()
+            src[cc, :half] = (src[cc, :half].astype(F32) + land[1].astype(F32)).astype(BF16)
+        side(src, dst, send, recv, k).start()
+
+    def reduce_sum(src, dst, send, recv):
         total = src[c].astype(F32)
-        for k in range(1, TP):
-            total = total + dst[lax.rem(c + k, TP)].astype(F32)
+        for k in (1, 2):
+            side(src, dst, send, recv, k).wait_recv()
+            total = total + dst[k - 1].astype(F32)
         return total
 
     def block(piece, at, core):
         if piece == OUT:
-            return b.wout.at[at, core]
+            return b.wout.at[c, at, core]
         if piece == DOWN:
             return b.wdown.at[at, core]
         return b.wcol.at[piece, at, :, core]
@@ -545,7 +692,7 @@
 
     def spread_recv(piece):
         for k in range(1, TP):
-            cc, dev = plane(TP - k)
+            cc, dev = plane(k)
             remote(
                 scol.at[piece, cc],
                 b.wcol.at[piece, z, cc, f],
@@ -560,16 +707,25 @@
     b.tsend[...] = nn(pick, tok[...]).reshape(nd, per, width).astype(BF16)
     b.csend[...] = nn(pick, cot[...]).reshape(nd, per, width).astype(BF16)
 
+    gw = width // 128
+    heads_in(wq, 0)
+    heads_in(wk, 1)
+    heads_in(wv, 2)
+    spot = lax.broadcasted_iota(jnp.int32, (gw, 128), 0) == (me * row_dev) // 128
+    spot = spot & ((lane // row_dev) == me % (128 // row_dev))
+
+    def gain_tile(gain):
+        g = gain[...].astype(F32)
+        return jnp.where(spot, jnp.concatenate([g] * (128 // row_dev), axis=1), 0.0)
+
+    gains[...] = jnp.concatenate([gain_tile(gain1), gain_tile(gain2)], axis=0).astype(BF16)
     pl.semaphore_wait(barrier, nd)
 
     all_peers(lambda to: gains, b.grecv, s.g_s, s.g_r)
     all_peers(lambda to: b.tsend.at[to], b.trecv, s.t_s, s.t_r)
     for k in range(1, TP):
         spread(QKV, k).start()
-    for piece in (QKV, GATE, UP):
-        b.wcol[piece, z, c, f] = scol[piece, c]
-    b.wout[z, f] = sout[...]
-    b.wdown[z, f] = sdown[...]
+    b.wcol[QKV, z, c, f] = scol[QKV, c]
     b.trecv[dp] = b.tsend[dp]
     b.crecv[dp] = b.csend[dp]
     b.grecv[dp] = gains[...]
@@ -585,9 +741,7 @@
     allowed = (seg_r == seg_c) & (ri >= ci) & (ri - ci < WINDOW)
     b.mask[c] = allowed.astype(F32).astype(BF16)
     gather_start(b.mask, s.m_s, s.m_r)
-    for piece in (GATE, UP):
-        for k in range(1, TP):
-            spread(piece, k).start()
+    rows_in(wo, b.wout.at[c, z, f], row_dev)
 
     all_peers_recv(lambda at: gains, b.grecv, s.g_s, s.g_r)
     gain_sum = jnp.sum(b.grecv[...].astype(F32), axis=0)
@@ -597,12 +751,17 @@
 
     spread_recv(QKV)
     line_start(QKV)
+    for piece, w in ((GATE, wg), (UP, wu)):
+        hidden_in(w, piece)
+        for k in range(1, TP):
+            spread(piece, k).start()
+        b.wcol[piece, z, c, f] = scol[piece, c]
+    rows_in(wd, b.wdown.at[z, f], PAD)
 
     all_peers_recv(lambda at: b.tsend.at[at], b.trecv, s.t_s, s.t_r)
     all_peers(lambda to: b.csend.at[to], b.crecv, s.c_s, s.c_r)
     remote(b.gpart.at[other], b.gpart.at[other], s.gb_s, s.gb_r, sib).wait_recv()
     gain_tile = b.gpart[0].astype(F32) + b.gpart[1].astype(F32)
-    gw = width // 128
     b.gain[0:1] = row_of(gain_tile[0:gw])
     b.gain[1:2] = row_of(gain_tile[gw : 2 * gw])
 
@@ -614,195 +773,275 @@
     line_step(QKV, 1)
     line_start(OUT)
     line_step(QKV, 2)
-    line_step(QKV, 3)
     spread_recv(GATE)
     spread_recv(UP)
     line_start(GATE)
+    line_step(QKV, 3)
     line_step(OUT, 1)
-    all_peers_recv(lambda at: b.csend.at[at], b.crecv, s.c_s, s.c_r)
-    b.call[c] = b.crecv[...].reshape(rows, width)
-    gather_recv(b.n1, s.a_s.at[0], s.a_r.at[0])
-    gather_start(b.call, s.a_s.at[1], s.a_r.at[1])
+    gather_recv(b.mask, s.m_s, s.m_r)
     line_done(QKV)
-    n1 = b.n1[...].reshape(toks, width)
-    for j in range(3):
-        w = b.wcol[QKV, :, :, :, :, j * hw : (j + 1) * hw].reshape(width, hw)
-        b.qkv[:, j * hw : (j + 1) * hw] = nn(n1, w).astype(BF16)
-    line_step(OUT, 2)
-    line_step(GATE, 1)
-    line_start(UP)
-    gather_recv(b.mask, s.m_s, s.m_r)
     scale = HEAD ** (-0.5)
 
-    @pl.loop(0, TP)
-    def _(i):
-        at = pl.ds(pl.multiple_of(i * rows, rows), rows)
-        blk = b.qkv[at, :]
+    def out_rows(cc, core):
+        return b.wout.at[cc, :, core]
+
+    def out_send(k):
+        _, dev = plane(k)
+        return remote(out_rows(c, f), out_rows(c, f), s.o_s.at[k], s.o_r.at[k], dev)
+
+    def out_mirror(k, core):
+        rows_of = out_rows(plane(k)[0], core)
+        return remote(rows_of, rows_of, s.om_s.at[k], s.om_r.at[k], sib)
+
+    def attend(k):
+        i = plane(k)[0]
+        if k:
+            gather_one(b.n1, k, s.a_s.at[0], s.a_r.at[0])
+        w = b.wcol[QKV].reshape(width, fw)
+        b.qkv[i] = nn(b.n1[i], w).astype(BF16)
+        blk = b.qkv[i]
         allow = b.mask[i].astype(F32) > 0.5
         outs = []
         for h in range(heads):
             q = blk[:, h * HEAD : (h + 1) * HEAD]
-            k = blk[:, hw + h * HEAD : hw + (h + 1) * HEAD]
+            key = blk[:, hw + h * HEAD : hw + (h + 1) * HEAD]
             v = blk[:, 2 * hw + h * HEAD : 2 * hw + (h + 1) * HEAD]
-            scores = jnp.where(allow, nt(q, k) * scale, -1e30)
+            scores = jnp.where(allow, nt(q, key) * scale, -1e30)
             e = jnp.exp(scores - jnp.max(scores, axis=1, keepdims=True))
             p = e / jnp.sum(e, axis=1, keepdims=True)
-            b.probs[i * heads + h] = p
+            b.probs[i, h] = p
             outs.append(nn(p.astype(BF16), v))
-        b.att[at, :] = jnp.concatenate(outs, axis=1).astype(BF16)
-
+        b.att[i] = jnp.concatenate(outs, axis=1).astype(BF16)
+        if k:
+            swap(b.att, b.attall, s.x_s.at[0], s.x_r.at[0], k).start()
+        else:
+            b.attall[c] = b.att[c]
+
+    attend(0)
+    line_step(OUT, 2)
+    attend(1)
     line_step(OUT, 3)
+    for k in range(1, TP):
+        out_send(k).start()
+    line_start(UP)
+    attend(2)
+    line_step(GATE, 1)
+    attend(3)
+    all_peers_recv(lambda at: b.csend.at[at], b.crecv, s.c_s, s.c_r)
+    b.call[c] = b.crecv[...].reshape(rows, width)
     line_step(GATE, 2)
-    line_step(UP, 1)
+    for k in range(1, TP):
+        cc, dev = plane(k)
+        remote(out_rows(c, f), out_rows(cc, f), s.o_s.at[k], s.o_r.at[k], dev).wait_recv()
+        out_mirror(k, f).start()
+    gather_start(b.call, s.a_s.at[1], s.a_r.at[1])
     line_done(OUT)
-    att = b.att[...]
-
-    @pl.loop(0, tiles)
-    def _(j):
-        cols = pl.ds(pl.multiple_of(j * tw, tw), tw)
-        w = b.wout[:, :, :, cols].reshape(hw, tw)
-        b.p[0][:, :, cols] = nn(att, w).reshape(TP, rows, tw).astype(BF16)
-        scatter_tile(b.p[0], b.q[0], s.r_s.at[0], s.r_r.at[0], j)
-
-    line_step(GATE, 3)
-    line_start(DOWN)
-    line_step(UP, 2)
-    scatter_recv(b.p[0], b.q[0], s.r_s.at[0], s.r_r.at[0])
-    middle = b.trecv[...].astype(F32).reshape(rows, width) + scatter_sum(b.p[0], b.q[0])
+    for k in range(1, TP):
+        out_mirror(k, other).wait_recv()
+        swap_recv(b.att, b.attall, s.x_s.at[0], s.x_r.at[0], k)
+    middle = b.trecv[...].astype(F32).reshape(rows, width)
+    for i in range(TP):
+        middle = middle + nn(b.attall[i], b.wout[i].reshape(hw, width))
     b.middle[...] = middle
     unit = middle * lax.rsqrt(jnp.mean(middle * middle, axis=1, keepdims=True) + EPSILON)
     b.n2[c] = (unit * b.gain[1:2]).astype(BF16)
     gather_start(b.n2, s.a_s.at[2], s.a_r.at[2])
+    line_step(GATE, 3)
+    line_step(UP, 1)
+    line_start(DOWN)
+    line_step(UP, 2)
     line_step(UP, 3)
-    line_step(DOWN, 1)
     line_done(GATE)
     line_done(UP)
-    gather_recv(b.n2, s.a_s.at[2], s.a_r.at[2])
-    n2 = b.n2[...].reshape(toks, width)
-    fb = 256
-    for j in range(fw // fb):
-        cols = slice(j * fb, (j + 1) * fb)
-        gate = nn(n2, b.wcol[GATE, :, :, :, :, cols].reshape(width, fb))
-        up = nn(n2, b.wcol[UP, :, :, :, :, cols].reshape(width, fb))
-        b.gate[:, cols] = gate
-        b.up[:, cols] = up
-        b.hid[:, cols] = (gate * jax.nn.sigmoid(gate) * up).astype(BF16)
-    line_step(DOWN, 2)
-
-    gather_recv(b.call, s.a_s.at[1], s.a_r.at[1])
-    call = b.call[...].reshape(toks, width)
+
+    def feed(k):
+        i = plane(k)[0]
+        if k:
+            gather_one(b.n2, k, s.a_s.at[2], s.a_r.at[2])
+        gate = nn(b.n2[i], b.wcol[GATE].reshape(width, fw))
+        up = nn(b.n2[i], b.wcol[UP].reshape(width, fw))
+        b.gate[i] = gate
+        b.up[i] = up
+        b.hid[i] = (gate * jax.nn.sigmoid(gate) * up).astype(BF16)
+
+    feed(0)
+    feed(1)
+    feed(2)
+    feed(3)
+    line_step(DOWN, 1)
 
     def presum(piece, src, dst):
         return remote(src, dst, s.p_s.at[piece], s.p_r.at[piece], sib)
 
-    def row_send(piece, src, dst, start):
-        for k in range(1, zn):
-            zz = lax.rem(z + k, zn)
-            cp = remote(
-                src.at[zz], dst.at[z], s.w_s.at[piece, k], s.w_r.at[piece, k], (zz * TP + c, f)
-            )
-            cp.start() if start else cp.wait_send()
-
-    def row_recv(piece, src, dst):
-        for k in range(1, zn):
-            zz = lax.rem(z + (zn - k), zn)
-            remote(
-                src.at[zz], dst.at[zz], s.w_s.at[piece, k], s.w_r.at[piece, k], (zz * TP + c, f)
-            ).wait_recv()
-
-    for j in range(fw // (4 * PAD)):
-        w = tn(b.hid[:, j * 4 * PAD : (j + 1) * 4 * PAD], call)
-        b.gdown[2 * j : 2 * j + 2] = w.reshape(2, CORES, PAD, width).astype(BF16)
-    presum(DOWN, b.gdown.at[:, other], b.cdown).start()
-    line_step(DOWN, 3)
-    line_done(DOWN)
-    for j in range(fw // (4 * PAD)):
-        cols = slice(j * 4 * PAD, (j + 1) * 4 * PAD)
-        gh = nt(call, b.wdown[2 * j : 2 * j + 2].reshape(4 * PAD, width))
-        gate = b.gate[:, cols]
-        sg = jax.nn.sigmoid(gate)
-        b.ggate[:, cols] = (gh * b.up[:, cols] * sg * (1.0 + gate * (1.0 - sg))).astype(BF16)
-        b.gup[:, cols] = (gh * gate * sg).astype(BF16)
-
-    presum(DOWN, b.gdown.at[:, f], b.cdown).wait_recv()
-    for at in range(zn):
-        b.sdown[at] = (b.gdown[at, f].astype(F32) + b.cdown[at].astype(F32)).astype(BF16)
-    row_send(DOWN, b.sdown, b.rdown, True)
-    b.rdown[z] = b.sdown[z]
-
-    @pl.loop(0, tiles)
-    def _(j):
-        cols = pl.ds(pl.multiple_of(j * tw, tw), tw)
-        v = nt(b.ggate[...], b.wcol[GATE, j].reshape(tw, fw))
-        v = v + nt(b.gup[...], b.wcol[UP, j].reshape(tw, fw))
-        b.p[1][:, :, cols] = v.reshape(TP, rows, tw).astype(BF16)
-        scatter_tile(b.p[1], b.q[1], s.r_s.at[1], s.r_r.at[1], j)
+    def part_of(piece):
+        if piece == OUT:
+            return b.gout.at[:, f], b.cout, b.sout, b.eout
+        if piece == DOWN:
+            return b.gdown.at[:, f], b.cdown, b.sdown, b.edown
+        return b.gcol.at[piece, :, :, f], b.ccol.at[piece], b.scol.at[piece], b.ecol.at[piece]
+
+    def half_of(piece):
+        if piece == OUT:
+            return b.gout.at[:, other]
+        if piece == DOWN:
+            return b.gdown.at[:, other]
+        return b.gcol.at[piece, :, :, other]
+
+    edge = (z == 0) | (z == zn - 1)
+
+    def travel(piece, at, slot, send, to):
+        _, _, part, land = part_of(piece)
+        return remote(
+            part.at[at], land.at[slot], s.e_s.at[piece, send], s.e_r.at[piece, slot], (to * TP + c, f)
+        )
+
+    inner = 1 + z // (zn - 1)
+    end = (z - 1) * (zn - 1)
+
+    def edge_send(piece, k):
+        at, slot = ((zn - 1 - z, 3), (zn - 1 - inner, 2), (inner, 0))[k]
+        return travel(piece, at, slot, slot, inner)
+
+    def inner_send(piece, k):
+        to, slot = ((end, 0), (zn - 1 - end, 1), (zn - 1 - z, 1))[k]
+        return travel(piece, to, slot, k, to)
+
+    def sum_start(piece):
+        mine, came, part, _ = part_of(piece)
+        presum(piece, half_of(piece), came).wait_recv()
+
+        @pl.loop(0, zn)
+        def _(j):
+            part[j] = (mine[j].astype(F32) + came[j].astype(F32)).astype(BF16)
+
+        @pl.when(edge)
+        def _():
+            for k in range(3):
+                edge_send(piece, k).start()
+
+        @pl.when(jnp.logical_not(edge))
+        def _():
+            inner_send(piece, 0).start()
+
+    def sum_middle(piece):
+        _, _, part, land = part_of(piece)
+
+        @pl.when(jnp.logical_not(edge))
+        def _():
+            for k, slot, at in ((1, 3, zn - 1 - end), (2, 2, zn - 1 - z)):
+                travel(piece, at, slot, slot, z).wait_recv()
+                part[at] = (part[at].astype(F32) + land[slot].astype(F32)).astype(BF16)
+                inner_send(piece, k).start()
+
+    def sum_end(piece):
+        _, _, part, land = part_of(piece)
+        for slot in (0, 1):
+            travel(piece, z, slot, slot, z).wait_recv()
+        return part[z].astype(F32) + land[0].astype(F32) + land[1].astype(F32)
+
+    def sum_sent(piece):
+        @pl.when(edge)
+        def _():
+            for k in range(3):
+                edge_send(piece, k).wait_send()
+
+        @pl.when(jnp.logical_not(edge))
+        def _():
+            for k in range(3):
+                inner_send(piece, k).wait_send()
+
+        presum(piece, half_of(piece), part_of(piece)[1]).wait_send()
 
     def col_grad(piece, act, grad):
         @pl.loop(0, zn)
         def _(j):
             a = act[:, :, pl.ds(pl.multiple_of(j * tw, tw), tw)].reshape(toks, tw)
-            g = tn(a, grad[...])
+            g = tn(a, grad[...].reshape(toks, fw))
             b.gcol[piece, j] = g.reshape(TP, CORES, row_dev, fw).astype(BF16)
 
-        presum(piece, b.gcol.at[piece, :, :, other], b.ccol.at[piece]).start()
-
-    def col_send(piece):
-        presum(piece, b.gcol.at[piece, :, :, f], b.ccol.at[piece]).wait_recv()
-
-        @pl.loop(0, zn)
-        def _(j):
-            v = b.gcol[piece, j, :, f].astype(F32) + b.ccol[piece, j].astype(F32)
-            b.scol[piece, j] = v.astype(BF16)
-
-        @pl.loop(1, nd)
-        def _(k):
-            to = lax.rem(dp + k, nd)
+        presum(piece, half_of(piece), b.ccol.at[piece]).start()
+
+    def home(piece, k):
+        cc, dev = plane(k)
+        return remote(
+            b.tcol.at[piece, cc], b.rcol.at[piece, c], s.h2_s.at[piece, k], s.h2_r.at[piece, k], dev
+        )
+
+    def col_end(piece):
+        b.tcol[piece] = sum_end(piece).astype(BF16)
+        for k in range(1, TP):
+            home(piece, k).start()
+        b.rcol[piece, c] = b.tcol[piece, c]
+
+    def my_gain(tile):
+        row = jnp.sum(jnp.where(spot, tile, 0.0), axis=0, keepdims=True)
+        total = row[:, :row_dev]
+        for k in range(1, 128 // row_dev):
+            total = total + row[:, k * row_dev : (k + 1) * row_dev]
+        return total
+
+    def col_recv(piece):
+        for k in range(1, TP):
+            cc, dev = plane(k)
             remote(
-                b.scol.at[piece, to // TP, to % TP],
-                b.rcol.at[piece, z, c],
-                s.w_s.at[piece, k],
-                s.w_r.at[piece, k],
-                (to, f),
-            ).start()
-
-        b.rcol[piece, z, c] = b.scol[piece, z, c]
-
-    def col_recv(piece):
-        @pl.loop(1, nd)
-        def _(k):
-            at = lax.rem(dp + (nd - k), nd)
-            remote(
-                b.scol.at[piece, z, c],
-                b.rcol.at[piece, at // TP, at % TP],
-                s.w_s.at[piece, k],
-                s.w_r.at[piece, k],
-                (at, f),
+                b.tcol.at[piece, cc], b.rcol.at[piece, cc], s.h2_s.at[piece, k], s.h2_r.at[piece, k], dev
             ).wait_recv()
 
-        total = b.rcol[piece, 0].astype(F32)
-        for k in range(1, zn):
-            total = total + b.rcol[piece, k].astype(F32)
-        ocol[piece] = total
-
-    def col_sent(piece):
-        @pl.loop(1, nd)
-        def _(k):
-            to = lax.rem(dp + k, nd)
-            remote(
-                b.scol.at[piece, to // TP, to % TP],
-                b.rcol.at[piece, z, c],
-                s.w_s.at[piece, k],
-                s.w_r.at[piece, k],
-                (to, f),
-            ).wait_send()
-
+    gather_recv(b.call, s.a_s.at[1], s.a_r.at[1])
+    call = b.call[...].reshape(toks, width)
+    span = 4 * PAD
+    for j in range(fw // span):
+        w = tn(b.hid[:, :, j * span : (j + 1) * span].reshape(toks, span), call)
+        b.gdown[2 * j : 2 * j + 2] = w.reshape(2, CORES, PAD, width).astype(BF16)
+    presum(DOWN, half_of(DOWN), b.cdown).start()
+    line_step(DOWN, 2)
+    sum_start(DOWN)
+    line_step(DOWN, 3)
+    line_done(DOWN)
+
+    def feed_back(k):
+        i = plane(k)[0]
+        gh = nt(b.call[i], b.wdown[...].reshape(fw, width))
+        gate = b.gate[i]
+        sg = jax.nn.sigmoid(gate)
+        b.ggate[i] = (gh * b.up[i] * sg * (1.0 + gate * (1.0 - sg))).astype(BF16)
+        b.gup[i] = (gh * gate * sg).astype(BF16)
+        v = nt(b.ggate[i], b.wcol[GATE].reshape(width, fw))
+        v = v + nt(b.gup[i], b.wcol[UP].reshape(width, fw))
+        b.p[1][i] = v.astype(BF16)
+
+    red1 = (b.p[1], b.q[1], b.land.at[1], s.x_s.at[1], s.x_r.at[1])
+    red0 = (b.p[0], b.q[0], b.land.at[0], s.x_s.at[3], s.x_r.at[3])
+    red2 = (b.p[2], b.q[2], b.land.at[2], s.x_s.at[4], s.x_r.at[4])
+
+    def red_start(red):
+        reduce_start(red[0], red[2], red[3], red[4])
+
+    def red_sum(red):
+        return reduce_sum(red[0], red[1], red[3], red[4])
+
+    feed_back(3)
+    red_start(red1)
+    feed_back(1)
+    reduce_side(*red1, 1)
+    feed_back(2)
+    reduce_side(*red1, 2)
+    feed_back(0)
     col_grad(GATE, b.n2, b.ggate)
+    sum_middle(DOWN)
     col_grad(UP, b.n2, b.gup)
-    col_send(GATE)
-
-    scatter_recv(b.p[1], b.q[1], s.r_s.at[1], s.r_r.at[1])
-    gn = scatter_sum(b.p[1], b.q[1])
+    sum_start(GATE)
+
+    def feed_out(k):
+        i = plane(k)[0]
+        b.p[0][i] = nn(b.hid[i], b.wdown[...].reshape(fw, width)).astype(BF16)
+
+    for k in (3, 1, 2, 0):
+        feed_out(k)
+    sum_start(UP)
+
+    gn = red_sum(red1)
+    red_start(red0)
     middle = b.middle[...]
     inv = lax.rsqrt(jnp.mean(middle * middle, axis=1, keepdims=True) + EPSILON)
     unit = middle * inv
@@ -810,68 +1049,60 @@
     a = gn * b.gain[1:2]
     gm = b.call[c].astype(F32) + inv * (a - unit * jnp.mean(a * unit, axis=1, keepdims=True))
     b.gmid[...] = gm
-    b.gb[c] = gm.astype(BF16)
-    gather_start(b.gb, s.a_s.at[3], s.a_r.at[3])
-    col_send(UP)
-
-    hid = b.hid[...]
-
-    @pl.loop(0, tiles)
-    def _(j):
-        cols = pl.ds(pl.multiple_of(j * tw, tw), tw)
-        w = b.wdown[:, :, :, cols].reshape(fw, tw)
-        b.p[2][:, :, cols] = nn(hid, w).reshape(TP, rows, tw).astype(BF16)
-        scatter_tile(b.p[2], b.q[2], s.r_s.at[2], s.r_r.at[2], j)
-
-    gather_recv(b.gb, s.a_s.at[3], s.a_r.at[3])
-    gb = b.gb[...].reshape(toks, width)
-    b.ga[...] = nt(gb, b.wout[...].reshape(hw, width)).astype(BF16)
-    b.gout[...] = tn(b.att[...], gb).reshape(zn, CORES, row_dev, width).astype(BF16)
-    presum(OUT, b.gout.at[:, other], b.cout).start()
-
-    @pl.loop(0, TP)
-    def _(i):
-        at = pl.ds(pl.multiple_of(i * rows, rows), rows)
-        blk = b.qkv[at, :]
-        gab = b.ga[at, :]
+    gb = gm.astype(BF16)
+    b.gb[c] = gb
+    for k in (3, 1, 2, 0):
+        i = plane(k)[0]
+        b.gasend[i] = nt(gb, b.wout[i].reshape(hw, width)).astype(BF16)
+        if k:
+            swap(b.gasend, b.ga, s.x_s.at[2], s.x_r.at[2], k).start()
+        else:
+            b.ga[c] = b.gasend[c]
+    reduce_side(*red0, 1)
+    reduce_side(*red0, 2)
+    sum_middle(GATE)
+
+    def attend_back(k):
+        i = plane(k)[0]
+        if k:
+            swap_recv(b.gasend, b.ga, s.x_s.at[2], s.x_r.at[2], k)
+        blk = b.qkv[i]
+        gab = b.ga[i]
         gq, gk, gv = [], [], []
         for h in range(heads):
             q = blk[:, h * HEAD : (h + 1) * HEAD]
-            k = blk[:, hw + h * HEAD : hw + (h + 1) * HEAD]
+            key = blk[:, hw + h * HEAD : hw + (h + 1) * HEAD]
             v = blk[:, 2 * hw + h * HEAD : 2 * hw + (h + 1) * HEAD]
             ga = gab[:, h * HEAD : (h + 1) * HEAD]
-            p = b.probs[i * heads + h]
+            p = b.probs[i, h]
             gp = nt(ga, v)
             gs = (p * (gp - jnp.sum(p * gp, axis=1, keepdims=True))).astype(BF16)
-            gq.append(nn(gs, k) * scale)
+            gq.append(nn(gs, key) * scale)
             gk.append(tn(gs, q) * scale)
             gv.append(tn(p.astype(BF16), ga))
-        b.gqkv[at, :] = jnp.concatenate(gq + gk + gv, axis=1).astype(BF16)
-
-    presum(OUT, b.gout.at[:, f], b.cout).wait_recv()
-    for at in range(zn):
-        b.sout[at] = (b.gout[at, f].astype(F32) + b.cout[at].astype(F32)).astype(BF16)
-    row_send(OUT, b.sout, b.rout, True)
-    b.rout[z] = b.sout[z]
-
-    @pl.loop(0, tiles)
-    def _(j):
-        cols = pl.ds(pl.multiple_of(j * tw, tw), tw)
-        v = nt(b.gqkv[...], b.wcol[QKV, j].reshape(tw, fw))
-        b.p[3][:, :, cols] = v.reshape(TP, rows, tw).astype(BF16)
-        scatter_tile(b.p[3], b.q[3], s.r_s.at[3], s.r_r.at[3], j)
-
+        b.gqkv[i] = jnp.concatenate(gq + gk + gv, axis=1).astype(BF16)
+        b.p[2][i] = nt(b.gqkv[i], b.wcol[QKV].reshape(width, fw)).astype(BF16)
+
+    attend_back(3)
+    red_start(red2)
+    relay_start(b.gb, s.a_s.at[3], s.a_r.at[3])
+    attend_back(1)
+    reduce_side(*red2, 1)
+    attend_back(2)
+    reduce_side(*red2, 2)
+    attend_back(0)
     col_grad(QKV, b.n1, b.gqkv)
-
-    scatter_recv(b.p[2], b.q[2], s.r_s.at[2], s.r_r.at[2])
-    res = b.middle[...] + scatter_sum(b.p[2], b.q[2])
+    sum_middle(UP)
+    sum_start(QKV)
+    relay_pass(b.gb, s.a_s.at[3], s.a_r.at[3])
+    rows_out(od, sum_end(DOWN))
+
+    res = b.middle[...] + red_sum(red0)
     b.lsend[...] = res.reshape(nd, per, width).astype(BF16)
-    col_send(QKV)
     all_peers(lambda to: b.lsend.at[to], b.lrecv, s.l_s, s.l_r)
     b.lrecv[dp] = b.lsend[dp]
 
-    scatter_recv(b.p[3], b.q[3], s.r_s.at[3], s.r_r.at[3])
-    gn = scatter_sum(b.p[3], b.q[3])
+    gn = red_sum(red2)
     x = b.trecv[...].astype(F32).reshape(rows, width)
     inv = lax.rsqrt(jnp.mean(x * x, axis=1, keepdims=True) + EPSILON)
     unit = x * inv
@@ -885,15 +1116,21 @@
     all_peers(lambda to: b.hsend, b.hrecv, s.h_s, s.h_r)
     b.hrecv[dp] = b.hsend[...]
 
+    relay_done(b.gb, s.a_s.at[3], s.a_r.at[3])
+    gb_all = b.gb[...].reshape(toks, width)
+    b.gout[...] = (
+        tn(b.att[...].reshape(toks, hw), gb_all).reshape(zn, CORES, row_dev, width).astype(BF16)
+    )
+    presum(OUT, half_of(OUT), b.cout).start()
+    sum_middle(QKV)
+    sum_start(OUT)
+
+    col_end(GATE)
     all_peers_recv(lambda at: b.lsend.at[at], b.lrecv, s.l_s, s.l_r)
     pick = b.pick[...]
     lout[...] = tn(pick, b.lrecv[...].reshape(rows, width)).astype(BF16)
-    row_recv(DOWN, b.sdown, b.rdown)
-    odown[...] = jnp.sum(b.rdown[...].astype(F32), axis=0)
-    col_recv(GATE)
-    col_recv(UP)
-    row_recv(OUT, b.sout, b.rout)
-    oout[...] = jnp.sum(b.rout[...].astype(F32), axis=0)
+    sum_middle(OUT)
+    col_end(UP)
     all_peers_recv(lambda at: b.hsend, b.hrecv, s.h_s, s.h_r)
     b.hpart[f] = jnp.sum(b.hrecv[...], axis=0)
     hmirror = remote(b.hpart.at[f], b.hpart.at[f], s.hb_s, s.hb_r, sib)
@@ -901,8 +1138,19 @@
     all_peers_recv(lambda at: b.isend.at[at], b.irecv, s.i_s, s.i_r)
     igrad[...] = tn(pick, b.irecv[...].reshape(rows, width)).astype(BF16)
     remote(b.hpart.at[other], b.hpart.at[other], s.hb_s, s.hb_r, sib).wait_recv()
-    ogain[...] = b.hpart[0] + b.hpart[1]
+    gain_sum = b.hpart[0] + b.hpart[1]
+    ogain1[...] = my_gain(gain_sum[:gw])
+    ogain2[...] = my_gain(gain_sum[gw:])
+    col_recv(GATE)
+    hidden_out(og, GATE)
+    col_end(QKV)
+    col_recv(UP)
+    hidden_out(ou, UP)
+    rows_out(oo, sum_end(OUT))
     col_recv(QKV)
+    heads_out(oq, 0)
+    heads_out(ok, 1)
+    heads_out(ov, 2)
 
     gmirror.wait_send()
     hmirror.wait_send()
@@ -913,21 +1161,26 @@
     all_peers_sent(lambda to: b.isend.at[to], b.irecv, s.i_s, s.i_r)
     all_peers_sent(lambda to: b.hsend, b.hrecv, s.h_s, s.h_r)
     gather_sent(b.mask, s.m_s, s.m_r)
-    for i, buf in enumerate((b.n1, b.call, b.n2, b.gb)):
+    for i, buf in enumerate((b.n1, b.call, b.n2)):
         gather_sent(buf, s.a_s.at[i], s.a_r.at[i])
-    for i in range(4):
-        scatter_sent(b.p[i], b.q[i], s.r_s.at[i], s.r_r.at[i])
-    for piece in (QKV, GATE, UP):
-        for k in range(1, TP):
+    for k in range(TP):
+        relay(b.gb, s.a_s.at[3], s.a_r.at[3], k).wait_send()
+    for src, dst, land, send, recv in (red0, red1, red2):
+        for k in (3, 0):
+            halves(src, land, send, recv, k).wait_send()
+        for k in (1, 2):
+            side(src, dst, send, recv, k).wait_send()
+    for k in range(1, TP):
+        swap(b.att, b.attall, s.x_s.at[0], s.x_r.at[0], k).wait_send()
+        swap(b.gasend, b.ga, s.x_s.at[2], s.x_r.at[2], k).wait_send()
+        out_send(k).wait_send()
+        out_mirror(k, f).wait_send()
+        for piece in (QKV, GATE, UP):
             spread(piece, k).wait_send()
-        presum(piece, b.gcol.at[piece, :, :, other], b.ccol.at[piece]).wait_send()
-        col_sent(piece)
-    presum(OUT, b.gout.at[:, other], b.cout).wait_send()
-    presum(DOWN, b.gdown.at[:, other], b.cdown).wait_send()
-    row_send(OUT, b.sout, b.rout, False)
-    row_send(DOWN, b.sdown, b.rdown, False)
+            home(piece, k).wait_send()
     for piece in (QKV, GATE, UP, OUT, DOWN):
         line_sent(piece)
+        sum_sent(piece)
 
 
 def _log2(n):
@@ -978,41 +1231,17 @@
     unit = hidden // pieces
     hw = width // TP
     fw = PAD * CORES * zn
-    me = lax.axis_index(("dp", "fsdp"))
-
-    def head_cols(w):
-        w = w.reshape(row_dev, zn, TP, HEAD)
-        return w.transpose(2, 0, 1, 3).reshape(TP, row_dev, hw)
-
-    def hidden_cols(w):
-        w = w.reshape(row_dev, zn, TP, CORES, unit)
-        w = jnp.pad(w, ((0, 0), (0, 0), (0, 0), (0, 0), (0, PAD - unit)))
-        return w.transpose(2, 0, 1, 3, 4).reshape(TP, row_dev, fw)
-
-    scol = jnp.stack(
-        [
-            jnp.concatenate([head_cols(w_query), head_cols(w_key), head_cols(w_value)], axis=2),
-            hidden_cols(w_gate),
-            hidden_cols(w_up),
-        ]
-    )
-    sout = w_out.reshape(row_dev, width)
-    sdown = jnp.pad(w_down.reshape(unit, width), ((0, PAD - unit), (0, 0)))
     gw = width // 128
-    lanes = jnp.arange(128)[None, :]
-    tile_rows = jnp.arange(gw)[:, None]
-    mine = (tile_rows == me * row_dev // 128) & (lanes // row_dev == me % (128 // row_dev))
-
-    def gain_tile(gain):
-        return jnp.where(mine, jnp.tile(gain, 128 // row_dev)[None, :], 0).astype(BF16)
-
-    gains = jnp.concatenate([gain_tile(norm1_gain), gain_tile(norm2_gain)], axis=0)
-
     toks = TP * rows
     per = rows // nd
     V = pltpu.VMEM
     bufs = dict(
         pick=V((rows, rows), BF16),
+        own=V((3, TP, row_dev, fw), BF16),
+        gown=V((2 * gw, 128), BF16),
+        flat=V((PAD * width // 128, 128), F32),
+        pairs=V((fw // 128, row_dev, 128), F32),
+        wide=V((TP, fw // 128, row_dev, 128), F32),
         tsend=V((nd, per, width), BF16),
         trecv=V((nd, per, width), BF16),
         csend=V((nd, per, width), BF16),
@@ -1030,40 +1259,45 @@
         hpart=V((CORES, 2 * gw, 128), F32),
         mask=V((TP, rows, rows), BF16),
         wcol=V((3, zn, TP, CORES, row_dev, fw), BF16),
-        wout=V((zn, CORES, row_dev, width), BF16),
+        wout=V((TP, zn, CORES, row_dev, width), BF16),
         wdown=V((zn, CORES, PAD, width), BF16),
         n1=V((TP, rows, width), BF16),
         n2=V((TP, rows, width), BF16),
         call=V((TP, rows, width), BF16),
         gb=V((TP, rows, width), BF16),
-        qkv=V((toks, 3 * hw), BF16),
-        probs=V((TP * hw // HEAD, rows, rows), F32),
-        att=V((toks, hw), BF16),
+        qkv=V((TP, rows, 3 * hw), BF16),
+        probs=V((TP, hw // HEAD, rows, rows), F32),
+        att=V((TP, rows, hw), BF16),
+        attall=V((TP, rows, hw), BF16),
+        gasend=V((TP, rows, hw), BF16),
         middle=V((rows, width), F32),
         gmid=V((rows, width), F32),
-        gate=V((toks, fw), F32),
-        up=V((toks, fw), F32),
-        hid=V((toks, fw), BF16),
-        ggate=V((toks, fw), BF16),
-        gup=V((toks, fw), BF16),
-        ga=V((toks, hw), BF16),
-        gqkv=V((toks, 3 * hw), BF16),
+        gate=V((TP, rows, fw), F32),
+        up=V((TP, rows, fw), F32),
+        hid=V((TP, rows, fw), BF16),
+        ggate=V((TP, rows, fw), BF16),
+        gup=V((TP, rows, fw), BF16),
+        ga=V((TP, rows, hw), BF16),
+        gqkv=V((TP, rows, 3 * hw), BF16),
         gcol=V((3, zn, TP, CORES, row_dev, fw), BF16),
         ccol=V((3, zn, TP, row_dev, fw), BF16),
         scol=V((3, zn, TP, row_dev, fw), BF16),
-        rcol=V((3, zn, TP, row_dev, fw), BF16),
+        ecol=V((3, 4, TP, row_dev, fw), BF16),
+        tcol=V((3, TP, row_dev, fw), BF16),
+        rcol=V((3, TP, row_dev, fw), BF16),
         gout=V((zn, CORES, row_dev, width), BF16),
         cout=V((zn, row_dev, width), BF16),
         sout=V((zn, row_dev, width), BF16),
-        rout=V((zn, row_dev, width), BF16),
+        eout=V((4, row_dev, width), BF16),
         gdown=V((zn, CORES, PAD, width), BF16),
         cdown=V((zn, PAD, width), BF16),
         sdown=V((zn, PAD, width), BF16),
-        rdown=V((zn, PAD, width), BF16),
+        edown=V((4, PAD, width), BF16),
     )
     bufs.update(
-        p=[V((TP, rows, width), BF16) for _ in range(4)],
-        q=[V((TP, rows, width), BF16) for _ in range(4)],
+        p=[V((TP, rows, width), BF16) for _ in range(3)],
+        q=[V((2, rows, width), BF16) for _ in range(3)],
+        land=V((3, 2, rows // 2, width), BF16),
     )
     S = pltpu.SemaphoreType.DMA
     each = S((nd,))
@@ -1094,66 +1328,84 @@
         b_r=S((5, zn)),
         a_s=S((4, TP)),
         a_r=S((4, TP)),
-        r_s=S((4, 4, TP)),
-        r_r=S((4, 4, TP)),
+        o_s=S((TP,)),
+        o_r=S((TP,)),
+        om_s=S((TP,)),
+        om_r=S((TP,)),
+        x_s=S((5, TP)),
+        x_r=S((5, TP)),
         p_s=S((5,)),
         p_r=S((5,)),
-        w_s=S((5, nd)),
-        w_r=S((5, nd)),
-    )
-    n_io = 8 + 6
+        e_s=S((5, 4)),
+        e_r=S((5, 4)),
+        h2_s=S((3, TP)),
+        h2_r=S((3, TP)),
+    )
+    n_io = 13 + 11
     spaces, shape_of = jax.tree.flatten((bufs, sems))
 
     def entry(*refs):
         io, rest = refs[:n_io], refs[n_io:]
         b, s = jax.tree.unflatten(shape_of, rest)
-        block_kernel((nd, zn, rows, width, hw, fw), *io, SimpleNamespace(**b), SimpleNamespace(**s))
+        block_kernel((nd, zn, rows, width, hw, fw, unit), *io, SimpleNamespace(**b), SimpleNamespace(**s))
 
     vm = pl.BlockSpec(memory_space=pltpu.VMEM)
     sm = pl.BlockSpec(memory_space=pltpu.SMEM)
-    lout, igrad, ocol, oout, odown, ogain = pl.pallas_call(
+    head_span = jax.ShapeDtypeStruct((row_dev * width // 128, 128), F32)
+    hidden_span = jax.ShapeDtypeStruct((unit * width // 128, 128), F32)
+    gain_span = jax.ShapeDtypeStruct((1, row_dev), F32)
+    row_block = jax.ShapeDtypeStruct((rows, width), BF16)
+
+    def lanes(v):
+        return v.reshape(-1, 128)
+
+    outs = pl.pallas_call(
         entry,
-        out_shape=(
-            jax.ShapeDtypeStruct((rows, width), BF16),
-            jax.ShapeDtypeStruct((rows, width), BF16),
-            jax.ShapeDtypeStruct((3, TP, row_dev, fw), F32),
-            jax.ShapeDtypeStruct((row_dev, width), F32),
-            jax.ShapeDtypeStruct((PAD, width), F32),
-            jax.ShapeDtypeStruct((2 * gw, 128), F32),
-        ),
-        in_specs=[vm, vm, vm, sm, vm, vm, vm, vm],
-        out_specs=(vm,) * 6,
+        out_shape=(row_block, row_block, gain_span)
+        + (head_span,) * 4
+        + (gain_span,)
+        + (hidden_span,) * 3,
+        in_specs=[vm, vm, vm, sm] + [vm] * 9,
+        out_specs=(vm,) * 11,
         scratch_shapes=spaces,
         compiler_params=pltpu.CompilerParams(
             collective_id=0, has_side_effects=True, vmem_limit_bytes=VMEM_BYTES
         ),
         name="block_fwd_bwd",
-    )(tokens, cotangent, dealing.reshape(1, rows), lengths, gains, scol, sout, sdown)
-
-    def head_rows(g):
-        g = g.reshape(TP, row_dev, zn, HEAD)
-        return g.transpose(1, 2, 0, 3).reshape(-1)
-
-    def hidden_rows(g):
-        g = g.reshape(TP, row_dev, zn, CORES, PAD)[..., :unit]
-        return g.transpose(1, 2, 0, 3, 4).reshape(-1)
-
-    def my_gain(tile):
-        return lax.dynamic_slice(tile.reshape(-1), (me * row_dev,), (row_dev,))
-
-    return (
-        lout,
-        igrad,
-        my_gain(ogain[:gw]),
-        head_rows(ocol[0, :, :, :hw]),
-        head_rows(ocol[0, :, :, hw : 2 * hw]),
-        head_rows(ocol[0, :, :, 2 * hw :]),
-        oout.reshape(-1),
-        my_gain(ogain[gw:]),
-        hidden_rows(ocol[1]),
-        hidden_rows(ocol[2]),
-        odown[:unit].reshape(-1),
-    )
+    )(
+        tokens,
+        cotangent,
+        dealing.reshape(1, rows),
+        lengths,
+        norm1_gain.reshape(1, row_dev),
+        norm2_gain.reshape(1, row_dev),
+        lanes(w_query),
+        lanes(w_key),
+        lanes(w_value),
+        lanes(w_out),
+        lanes(w_gate),
+        lanes(w_up),
+        lanes(w_down),
+    )
+    whole = pl.BlockSpec(memory_space=pl.ANY)
+
+    def hand_over(*refs):
+        n = len(refs) // 2
+        copies = [pltpu.make_async_copy(refs[i], refs[n + i], refs[-1].at[i]) for i in range(n)]
+        for cp in copies:
+            cp.start()
+        for cp in copies:
+            cp.wait()
+
+    outs = pl.pallas_call(
+        hand_over,
+        out_shape=tuple(jax.ShapeDtypeStruct(v.shape, v.dtype) for v in outs),
+        in_specs=[vm] * len(outs),
+        out_specs=(whole,) * len(outs),
+        scratch_shapes=[S((len(outs),))],
+        name="hand_over",
+    )(*outs)
+    return tuple(outs[:2]) + tuple(v.reshape(-1) for v in outs[2:])
 
 
 def dispatch(dp_count, core_count, *args):

time: 207 us -> 172 us (0.83)
  local copies, waits for them, and re-layouts: 24.6 us -> 0 us
  Pallas kernels: 179 us -> 171 us
    reshape x17 -> x0, local copies, waits for them, and re-layouts: 12.8 us -> none  [the longest x2 2.98 us: hidden_rows(): return g.transpose(1, 2, 0, 3, 4).reshape(-1)]
    pallas_call x1 -> x2, Pallas kernels: 179 us -> 171 us  [the longest x1 168 us: planned(): pl.pallas_call(entry, out_shape=(row_block, row_block, gain_span) + (head...]
    another operation x12 -> x0, local copies, waits for them, and re-layouts: 4.02 us -> none  [the longest x2 1.32 us: gain_tile(): jnp.tile(gain, 128 // row_dev)[None, :]]
    unnamed x17 -> x0, local copies, waits for them, and re-layouts: 3.02 us -> none
where the time goes in v2:
time: 172 us
  Pallas kernels  171 us (99%)
    pallas_call x1, Pallas kernels, planned(): pl.pallas_call(entry, out_shape=(row_block, row_block, gain_span) + (head...  168 us

profile of v2, /device:TPU:0, one launch (start us, length us, event | category | flops | bytes accessed | tf_op | source)
XLA Modules:
  0.0 172.2 jit_solution(13162015837580591550)
XLA Ops:
  1.3 167.7 %block_fwd_bwd.1 = (bf16[128,1024]{1,0:T(8,128)(2,1)}, bf16[128,1024]{1,0:T(8,128)(2,1)}, f32[1,32]{1,0:T(1,128)}, f32[256,128]{1,0:T(8,128)}, f32[256,128]{1,0:...) custom-call(bf16[128,1024]{1,0:T(8,128)(2,1)} %refs_0_.1, ...), custom_call_target="tpu_custom_call" | custom-call | tf_op jit(solution)/shard_map/block_fwd_bwd/pallas_call | solution.py:1362
  169.0 3.0 %hand_over.1 = (bf16[128,1024]{1,0:T(8,128)(2,1)}, bf16[128,1024]{1,0:T(8,128)(2,1)}, f32[1,32]{1,0:T(1,128)}, f32[256,128]{1,0:T(8,128)}, f32[256,128]{1,0:T(8,...) custom-call(bf16[128,1024]{1,0:T(8,128)(2,1)} %get-tuple-element.33., ...), custom_call_target="tpu_custom_call" | custom-call | tf_op jit(solution)/shard_map/hand_over/pallas_call | solution.py:1400

commit v3 on v2

--- a/solution.py
+++ b/solution.py
@@ -536,10 +536,6 @@
     tiles = 4
     tw = width // tiles
 
-    def gather_one(buf, k, send, recv):
-        cc, dev = plane(k)
-        remote(buf.at[c], buf.at[cc], send.at[k], recv.at[k], dev).wait_recv()
-
     def swap(src, dst, send, recv, k):
         cc, dev = plane(k)
         return remote(src.at[cc], dst.at[c], send.at[k], recv.at[k], dev)
@@ -551,29 +547,35 @@
     half = rows // 2
     low, high = pl.ds(0, half), pl.ds(half, half)
 
-    def relay(buf, send, recv, k):
-        at = (plane(2)[0], c, c, plane(1)[0])[k]
-        ref = (buf.at[at, high], buf.at[at], buf.at[at], buf.at[at, low])[k]
+    def rows_part(buf):
+        def get(at, part):
+            return buf.at[at] if part is None else buf.at[at, (low, high)[part]]
+
+        return get
+
+    def relay_refs(get, send, recv, k, at):
+        ref = get(at, (1, None, None, 0)[k])
         return remote(ref, ref, send.at[k], recv.at[k], plane((1, 1, 2, 2)[k])[1])
 
-    def relay_wait(buf, send, recv, k):
-        at = plane((3, 1, 2, 3)[k])[0]
-        ref = (buf.at[at, high], buf.at[at], buf.at[at], buf.at[at, low])[k]
-        remote(ref, ref, send.at[k], recv.at[k], plane((1, 1, 2, 2)[k])[1]).wait_recv()
-
-    def relay_start(buf, send, recv):
-        relay(buf, send, recv, 1).start()
-        relay(buf, send, recv, 2).start()
-
-    def relay_pass(buf, send, recv):
-        relay_wait(buf, send, recv, 1)
-        relay(buf, send, recv, 3).start()
-        relay_wait(buf, send, recv, 2)
-        relay(buf, send, recv, 0).start()
-
-    def relay_done(buf, send, recv):
-        relay_wait(buf, send, recv, 3)
-        relay_wait(buf, send, recv, 0)
+    def relay(get, send, recv, k):
+        return relay_refs(get, send, recv, k, (plane(2)[0], c, c, plane(1)[0])[k])
+
+    def relay_wait(get, send, recv, k):
+        relay_refs(get, send, recv, k, plane((3, 1, 2, 3)[k])[0]).wait_recv()
+
+    def relay_start(get, send, recv):
+        relay(get, send, recv, 1).start()
+        relay(get, send, recv, 2).start()
+
+    def relay_pass(get, send, recv):
+        relay_wait(get, send, recv, 1)
+        relay(get, send, recv, 3).start()
+        relay_wait(get, send, recv, 2)
+        relay(get, send, recv, 0).start()
+
+    def relay_done(get, send, recv):
+        relay_wait(get, send, recv, 3)
+        relay_wait(get, send, recv, 0)
 
     def halves(src, land, send, recv, k):
         at = plane(3)[0]
@@ -630,52 +632,56 @@
             sib,
         )
 
+    own_hops = ((1, 0), (-1, 1), (2, 2), (-2, 3))
+
+    def reaches(by):
+        return z + by < zn if by > 0 else z + by >= 0
+
     def line_start(piece):
-        @pl.when(z < zn - 1)
-        def _():
-            hop(piece, z, 0, z + 1).start()
-
-        @pl.when(z > 0)
-        def _():
-            hop(piece, z, 1, z - 1).start()
+        for by, slot in own_hops:
+
+            @pl.when(reaches(by))
+            def _():
+                hop(piece, z, slot, z + by).start()
 
         mirror(piece, z, f).start()
 
-    def line_step(piece, d):
-        @pl.when(z >= d)
-        def _():
-            hop(piece, z - d, 0, z).wait_recv()
-
-            @pl.when(z < zn - 1)
+    def line_pass(piece):
+        for at_z, at, slot, to in ((zn - 2, 0, 4, zn - 1), (1, zn - 1, 5, 0)):
+
+            @pl.when(z == at_z)
             def _():
-                hop(piece, z - d, 2 * d, z + 1).start()
-
-            mirror(piece, z - d, f).start()
-
-        @pl.when(z + d < zn)
-        def _():
-            hop(piece, z + d, 0, z).wait_recv()
-
-            @pl.when(z > 0)
-            def _():
-                hop(piece, z + d, 2 * d + 1, z - 1).start()
-
-            mirror(piece, z + d, f).start()
+                hop(piece, at, slot, z).wait_recv()
+                hop(piece, at, slot, to).start()
+
+    def line_take(piece):
+        for d in range(1, zn):
+            for by, passer in ((-d, zn - 2), (d, 1)):
+
+                @pl.when(reaches(by) & ((z != passer) if d == zn - 2 else True))
+                def _():
+                    hop(piece, z + by, 0, z).wait_recv()
+
+                @pl.when(reaches(by))
+                def _():
+                    mirror(piece, z + by, f).start()
 
     def line_done(piece):
         for at in range(zn):
             mirror(piece, at, other).wait_recv()
 
     def line_sent(piece):
-        for d in range(zn):
-
-            @pl.when((z >= d) & (z < zn - 1))
+        for by, slot in own_hops:
+
+            @pl.when(reaches(by))
             def _():
-                hop(piece, z - d, 2 * d, z + 1).wait_send()
-
-            @pl.when((z + d < zn) & (z > 0))
+                hop(piece, z, slot, z + by).wait_send()
+
+        for at_z, at, slot, to in ((zn - 2, 0, 4, zn - 1), (1, zn - 1, 5, 0)):
+
+            @pl.when(z == at_z)
             def _():
-                hop(piece, z + d, 2 * d + 1, z - 1).wait_send()
+                hop(piece, at, slot, to).wait_send()
 
         for at in range(zn):
             mirror(piece, at, f).wait_send()
@@ -751,6 +757,7 @@
 
     spread_recv(QKV)
     line_start(QKV)
+    line_start(OUT)
     for piece, w in ((GATE, wg), (UP, wu)):
         hidden_in(w, piece)
         for k in range(1, TP):
@@ -768,35 +775,36 @@
     x = b.trecv[...].astype(F32).reshape(rows, width)
     unit = x * lax.rsqrt(jnp.mean(x * x, axis=1, keepdims=True) + EPSILON)
     b.n1[c] = (unit * b.gain[0:1]).astype(BF16)
-    gather_start(b.n1, s.a_s.at[0], s.a_r.at[0])
-
-    line_step(QKV, 1)
-    line_start(OUT)
-    line_step(QKV, 2)
+    n1_way = (rows_part(b.n1), s.a_s.at[0], s.a_r.at[0])
+    call_way = (rows_part(b.call), s.a_s.at[1], s.a_r.at[1])
+    n2_way = (rows_part(b.n2), s.a_s.at[2], s.a_r.at[2])
+    gb_way = (rows_part(b.gb), s.a_s.at[3], s.a_r.at[3])
+    relay_start(*n1_way)
+    line_pass(QKV)
     spread_recv(GATE)
+    line_start(GATE)
+    relay_pass(*n1_way)
     spread_recv(UP)
-    line_start(GATE)
-    line_step(QKV, 3)
-    line_step(OUT, 1)
+    line_pass(OUT)
+    line_take(QKV)
     gather_recv(b.mask, s.m_s, s.m_r)
+    line_start(UP)
     line_done(QKV)
     scale = HEAD ** (-0.5)
 
-    def out_rows(cc, core):
-        return b.wout.at[cc, :, core]
-
-    def out_send(k):
-        _, dev = plane(k)
-        return remote(out_rows(c, f), out_rows(c, f), s.o_s.at[k], s.o_r.at[k], dev)
+    def out_part(at, part):
+        return b.wout.at[at, :, f] if part is None else b.wout.at[at, pl.ds(part * (zn // 2), zn // 2), f]
+
+    out_way = (out_part, s.o_s, s.o_r)
 
     def out_mirror(k, core):
-        rows_of = out_rows(plane(k)[0], core)
+        rows_of = b.wout.at[plane(k)[0], :, core]
         return remote(rows_of, rows_of, s.om_s.at[k], s.om_r.at[k], sib)
 
     def attend(k):
         i = plane(k)[0]
-        if k:
-            gather_one(b.n1, k, s.a_s.at[0], s.a_r.at[0])
+        if k == 3:
+            relay_done(*n1_way)
         w = b.wcol[QKV].reshape(width, fw)
         b.qkv[i] = nn(b.n1[i], w).astype(BF16)
         blk = b.qkv[i]
@@ -817,47 +825,44 @@
         else:
             b.attall[c] = b.att[c]
 
+    attend(1)
+    line_take(OUT)
+    relay_start(*out_way)
+    attend(2)
+    attend(3)
+    line_pass(GATE)
     attend(0)
-    line_step(OUT, 2)
-    attend(1)
-    line_step(OUT, 3)
-    for k in range(1, TP):
-        out_send(k).start()
-    line_start(UP)
-    attend(2)
-    line_step(GATE, 1)
-    attend(3)
+    line_start(DOWN)
+    relay_pass(*out_way)
     all_peers_recv(lambda at: b.csend.at[at], b.crecv, s.c_s, s.c_r)
     b.call[c] = b.crecv[...].reshape(rows, width)
-    line_step(GATE, 2)
+    for k in (1, 2):
+        out_mirror(k, f).start()
+    line_done(OUT)
+    line_pass(UP)
+    relay_done(*out_way)
+    out_mirror(3, f).start()
     for k in range(1, TP):
-        cc, dev = plane(k)
-        remote(out_rows(c, f), out_rows(cc, f), s.o_s.at[k], s.o_r.at[k], dev).wait_recv()
-        out_mirror(k, f).start()
-    gather_start(b.call, s.a_s.at[1], s.a_r.at[1])
-    line_done(OUT)
-    for k in range(1, TP):
+        swap_recv(b.att, b.attall, s.x_s.at[0], s.x_r.at[0], k)
         out_mirror(k, other).wait_recv()
-        swap_recv(b.att, b.attall, s.x_s.at[0], s.x_r.at[0], k)
     middle = b.trecv[...].astype(F32).reshape(rows, width)
     for i in range(TP):
         middle = middle + nn(b.attall[i], b.wout[i].reshape(hw, width))
     b.middle[...] = middle
     unit = middle * lax.rsqrt(jnp.mean(middle * middle, axis=1, keepdims=True) + EPSILON)
     b.n2[c] = (unit * b.gain[1:2]).astype(BF16)
-    gather_start(b.n2, s.a_s.at[2], s.a_r.at[2])
-    line_step(GATE, 3)
-    line_step(UP, 1)
-    line_start(DOWN)
-    line_step(UP, 2)
-    line_step(UP, 3)
+    relay_start(*n2_way)
+    line_take(GATE)
+    relay_pass(*n2_way)
+    relay_start(*call_way)
+    line_take(UP)
     line_done(GATE)
     line_done(UP)
 
     def feed(k):
         i = plane(k)[0]
-        if k:
-            gather_one(b.n2, k, s.a_s.at[2], s.a_r.at[2])
+        if k == 3:
+            relay_done(*n2_way)
         gate = nn(b.n2[i], b.wcol[GATE].reshape(width, fw))
         up = nn(b.n2[i], b.wcol[UP].reshape(width, fw))
         b.gate[i] = gate
@@ -867,8 +872,9 @@
     feed(0)
     feed(1)
     feed(2)
+    relay_pass(*call_way)
     feed(3)
-    line_step(DOWN, 1)
+    line_pass(DOWN)
 
     def presum(piece, src, dst):
         return remote(src, dst, s.p_s.at[piece], s.p_r.at[piece], sib)
@@ -987,16 +993,15 @@
                 b.tcol.at[piece, cc], b.rcol.at[piece, cc], s.h2_s.at[piece, k], s.h2_r.at[piece, k], dev
             ).wait_recv()
 
-    gather_recv(b.call, s.a_s.at[1], s.a_r.at[1])
+    relay_done(*call_way)
     call = b.call[...].reshape(toks, width)
     span = 4 * PAD
     for j in range(fw // span):
         w = tn(b.hid[:, :, j * span : (j + 1) * span].reshape(toks, span), call)
         b.gdown[2 * j : 2 * j + 2] = w.reshape(2, CORES, PAD, width).astype(BF16)
     presum(DOWN, half_of(DOWN), b.cdown).start()
-    line_step(DOWN, 2)
     sum_start(DOWN)
-    line_step(DOWN, 3)
+    line_take(DOWN)
     line_done(DOWN)
 
     def feed_back(k):
@@ -1085,7 +1090,7 @@
 
     attend_back(3)
     red_start(red2)
-    relay_start(b.gb, s.a_s.at[3], s.a_r.at[3])
+    relay_start(*gb_way)
     attend_back(1)
     reduce_side(*red2, 1)
     attend_back(2)
@@ -1094,7 +1099,7 @@
     col_grad(QKV, b.n1, b.gqkv)
     sum_middle(UP)
     sum_start(QKV)
-    relay_pass(b.gb, s.a_s.at[3], s.a_r.at[3])
+    relay_pass(*gb_way)
     rows_out(od, sum_end(DOWN))
 
     res = b.middle[...] + red_sum(red0)
@@ -1116,7 +1121,7 @@
     all_peers(lambda to: b.hsend, b.hrecv, s.h_s, s.h_r)
     b.hrecv[dp] = b.hsend[...]
 
-    relay_done(b.gb, s.a_s.at[3], s.a_r.at[3])
+    relay_done(*gb_way)
     gb_all = b.gb[...].reshape(toks, width)
     b.gout[...] = (
         tn(b.att[...].reshape(toks, hw), gb_all).reshape(zn, CORES, row_dev, width).astype(BF16)
@@ -1161,10 +1166,9 @@
     all_peers_sent(lambda to: b.isend.at[to], b.irecv, s.i_s, s.i_r)
     all_peers_sent(lambda to: b.hsend, b.hrecv, s.h_s, s.h_r)
     gather_sent(b.mask, s.m_s, s.m_r)
-    for i, buf in enumerate((b.n1, b.call, b.n2)):
-        gather_sent(buf, s.a_s.at[i], s.a_r.at[i])
     for k in range(TP):
-        relay(b.gb, s.a_s.at[3], s.a_r.at[3], k).wait_send()
+        for way in (n1_way, call_way, n2_way, gb_way, out_way):
+            relay(*way, k).wait_send()
     for src, dst, land, send, recv in (red0, red1, red2):
         for k in (3, 0):
             halves(src, land, send, recv, k).wait_send()
@@ -1173,7 +1177,6 @@
     for k in range(1, TP):
         swap(b.att, b.attall, s.x_s.at[0], s.x_r.at[0], k).wait_send()
         swap(b.gasend, b.ga, s.x_s.at[2], s.x_r.at[2], k).wait_send()
-        out_send(k).wait_send()
         out_mirror(k, f).wait_send()
         for piece in (QKV, GATE, UP):
             spread(piece, k).wait_send()

time: 172 us -> 170 us (0.988)
  Pallas kernels: 171 us -> 168 us
    pallas_call x1, Pallas kernels: 168 us -> 165 us  [planned(): pl.pallas_call(entry, out_shape=(row_block, row_block, gain_span) + (head...]
where the time goes in v3:
time: 170 us; the launch traced here: 169 us
  Pallas kernels  168 us (99%)
    pallas_call x1, Pallas kernels, planned(): pl.pallas_call(entry, out_shape=(row_block, row_block, gain_span) + (head...  165 us

profile of v3, /device:TPU:0, one launch (start us, length us, event | category | flops | bytes accessed | tf_op | source)
XLA Modules:
  0.0 169.4 jit_solution(14448745418380022421)
XLA Ops:
  1.3 165.0 %block_fwd_bwd.1 = (bf16[128,1024]{1,0:T(8,128)(2,1)}, bf16[128,1024]{1,0:T(8,128)(2,1)}, f32[1,32]{1,0:T(1,128)}, f32[256,128]{1,0:T(8,128)}, f32[256,128]{1,0:...) custom-call(bf16[128,1024]{1,0:T(8,128)(2,1)} %refs_0_.1, ...), custom_call_target="tpu_custom_call" | custom-call | tf_op jit(solution)/shard_map/block_fwd_bwd/pallas_call | solution.py:1365
  166.3 3.0 %hand_over.1 = (bf16[128,1024]{1,0:T(8,128)(2,1)}, bf16[128,1024]{1,0:T(8,128)(2,1)}, f32[1,32]{1,0:T(1,128)}, f32[256,128]{1,0:T(8,128)}, f32[256,128]{1,0:T(8,...) custom-call(bf16[128,1024]{1,0:T(8,128)(2,1)} %get-tuple-element.33., ...), custom_call_target="tpu_custom_call" | custom-call | tf_op jit(solution)/shard_map/hand_over/pallas_call | solution.py:1403

commit v4 on v3

--- a/solution.py
+++ b/solution.py
@@ -1102,10 +1102,6 @@
     relay_pass(*gb_way)
     rows_out(od, sum_end(DOWN))
 
-    res = b.middle[...] + red_sum(red0)
-    b.lsend[...] = res.reshape(nd, per, width).astype(BF16)
-    all_peers(lambda to: b.lsend.at[to], b.lrecv, s.l_s, s.l_r)
-    b.lrecv[dp] = b.lsend[dp]
 
     gn = red_sum(red2)
     x = b.trecv[...].astype(F32).reshape(rows, width)
@@ -1121,6 +1117,10 @@
     all_peers(lambda to: b.hsend, b.hrecv, s.h_s, s.h_r)
     b.hrecv[dp] = b.hsend[...]
 
+    res = b.middle[...] + red_sum(red0)
+    b.lsend[...] = res.reshape(nd, per, width).astype(BF16)
+    all_peers(lambda to: b.lsend.at[to], b.lrecv, s.l_s, s.l_r)
+    b.lrecv[dp] = b.lsend[dp]
     relay_done(*gb_way)
     gb_all = b.gb[...].reshape(toks, width)
     b.gout[...] = (

time: 170 us -> 170 us (level)
  no operation moved by 1% of the time
where the time goes in v4:
time: 170 us; the launch traced here: 169 us
  Pallas kernels  167 us (98%)
    pallas_call x1, Pallas kernels, planned(): pl.pallas_call(entry, out_shape=(row_block, row_block, gain_span) + (head...  164 us

profile of v4, /device:TPU:0, one launch (start us, length us, event | category | flops | bytes accessed | tf_op | source)
XLA Modules:
  0.0 168.7 jit_solution(4558400925216729188)
XLA Ops:
  1.3 164.2 %block_fwd_bwd.1 = (bf16[128,1024]{1,0:T(8,128)(2,1)}, bf16[128,1024]{1,0:T(8,128)(2,1)}, f32[1,32]{1,0:T(1,128)}, f32[256,128]{1,0:T(8,128)}, f32[256,128]{1,0:...) custom-call(bf16[128,1024]{1,0:T(8,128)(2,1)} %refs_0_.1, ...), custom_call_target="tpu_custom_call" | custom-call | tf_op jit(solution)/shard_map/block_fwd_bwd/pallas_call | solution.py:1365
  165.5 3.0 %hand_over.1 = (bf16[128,1024]{1,0:T(8,128)(2,1)}, bf16[128,1024]{1,0:T(8,128)(2,1)}, f32[1,32]{1,0:T(1,128)}, f32[256,128]{1,0:T(8,128)}, f32[256,128]{1,0:T(8,...) custom-call(bf16[128,1024]{1,0:T(8,128)(2,1)} %get-tuple-element.33., ...), custom_call_target="tpu_custom_call" | custom-call | tf_op jit(solution)/shard_map/hand_over/pallas_call | solution.py:1403
